TPU v7x, 256 devices: a whole 4x4x8 slice. The times are simulated.
256 devices in a mesh: mom: 16 (over z, core), bond: 16 (over y, x).
Axes of the slice: x: 4, y: 4, z: 8, core: 2. Of those that a mesh axis runs over, the one named last changes fastest.
Arguments:
- vertex: bfloat16 [3, 256, 512, 512], P(None, ('mom', 'bond')), may hold values from -6 to 6
- loop_matrix: bfloat16 [3, 256, 512, 512], P(None, ('mom', 'bond')), may hold values from -0.01171875 to 0.01171875
- own_mix: float32 [3, 3], replicated, may hold values from -4 to 4
- cross_mix: float32 [3, 3], replicated, may hold values from -4 to 4
- shells: int32 [512], replicated, may hold values from 0 to 4
- partner: int32 [512], replicated, may hold values from 0 to 511, as said below
- grid_index: int32 [256], replicated, may hold values from 0 to 255, each once
Outputs:
- flowed: bfloat16 [3, 256, 512, 512], P(None, ('mom', 'bond'))
Inputs may be any that keep to these rules, and one draw needn't show every extreme that they name: partner[partner[a]] = a and partner[a] != a for every bond a; partner[a] // 32 = (a // 32 + 512 // 64) % 16. `grid_index`: each grid point appears once; point k has coordinates (k // 16, k % 16).
All inputs are finite; a program needn't handle non-finite values.
Results may differ from a plain program's by a relative error of at most 0.007.
Values may be sent and summed in bfloat16 or wider, within the bound.
No kernel may reach another device: no remote copies, remote signals or barrier semaphores. Data moves between devices by JAX's collectives and lax.ppermute only.
A program may use at most 128 MiB of HBM per device.

v0:
```python
import math

import jax
import jax.numpy as jnp
from jax import lax
from jax.sharding import PartitionSpec as P

G = 16
NB = 512
Q = 256


def from_partner(x, axis, bit):
    return lax.ppermute(x, axis, [(i, i ^ 1 << bit) for i in range(lax.axis_size(axis))])


def cas_table(grid_index, negate):
    points = jnp.arange(Q, dtype=jnp.int32)
    disp_x = points // G
    disp_y = points % G
    wave_x = grid_index // G
    wave_y = grid_index % G
    phases = (disp_x[:, None] * wave_x[None, :] + disp_y[:, None] * wave_y[None, :]) % G
    if negate:
        phases = (G - phases) % G
    angles = phases.astype(jnp.float32) * (2.0 * math.pi / G)
    return (jnp.cos(angles) + jnp.sin(angles)).astype(jnp.bfloat16)


def cycle_index():
    points = jnp.arange(Q, dtype=jnp.int32)
    centre_x = (points // G + G // 2) % G - G // 2
    centre_y = (points % G + G // 2) % G - G // 2
    return jnp.maximum(jnp.abs(centre_x), jnp.abs(centre_y))


def per_device(vertex, loop_matrix, own_mix, cross_mix, shells, partner, grid_index):
    mom_count = lax.axis_size("mom")
    bond_count = lax.axis_size("bond")
    channels = vertex.shape[0]
    mom_local = vertex.shape[1]
    row_block = NB // mom_count
    col_block = NB // bond_count
    entries = row_block * col_block
    mom_place = lax.axis_index("mom")
    bond_place = lax.axis_index("bond")
    half_product = jnp.einsum(
        "cqab,cqbd->cqad", vertex, loop_matrix, preferred_element_type=jnp.float32
    ).astype(jnp.bfloat16)
    product = jnp.einsum(
        "cqab,cqbd->cqad", half_product, vertex, preferred_element_type=jnp.float32
    )
    rounded = product.astype(jnp.bfloat16)
    depth_count = rounded.shape[0]
    shaped = rounded.reshape(depth_count, mom_local, mom_count, row_block, bond_count, col_block)
    arrived_blocks = lax.all_to_all(
        lax.all_to_all(
            shaped.transpose(0, 2, 4, 1, 3, 5).reshape(
                depth_count, mom_count, bond_count, mom_local, entries
            ),
            "mom",
            split_axis=1,
            concat_axis=3,
            tiled=True,
        ),
        "bond",
        split_axis=2,
        concat_axis=3,
        tiled=True,
    )
    blocks = arrived_blocks.reshape(channels, Q, entries)
    mirrored = from_partner(blocks, "mom", mom_count.bit_length() - 2)
    mirrored = from_partner(mirrored, "bond", bond_count.bit_length() - 2)
    row_index = lax.dynamic_slice_in_dim(partner, mom_place * row_block, row_block) % row_block
    col_index = lax.dynamic_slice_in_dim(partner, bond_place * col_block, col_block) % col_block
    flat_index = (row_index[:, None] * col_block + col_index[None, :]).reshape(entries)
    crossed = jnp.take(mirrored, flat_index, axis=2)
    local_grid = grid_index.reshape(mom_count, bond_count, mom_local).transpose(1, 0, 2).reshape(Q)
    plus_table = cas_table(local_grid, False)
    minus_table = cas_table(local_grid, True)
    own_lattice = jnp.einsum("rq,cqe->cre", plus_table, blocks, preferred_element_type=jnp.float32)
    cross_lattice = jnp.einsum(
        "rq,cqe->cre", minus_table, crossed, preferred_element_type=jnp.float32
    )
    mixed_terms = jnp.einsum(
        "dc,cre->dre", own_mix, own_lattice, precision=lax.Precision.HIGHEST
    ) + jnp.einsum("dc,cre->dre", cross_mix, cross_lattice, precision=lax.Precision.HIGHEST)
    shell_rows = lax.dynamic_slice_in_dim(shells, mom_place * row_block, row_block)
    shell_cols = lax.dynamic_slice_in_dim(shells, bond_place * col_block, col_block)
    reach_sum = (shell_rows[:, None] + shell_cols[None, :]).reshape(entries)
    kept_mask = cycle_index()[:, None] <= reach_sum[None, :]
    projected = jnp.where(kept_mask[None], mixed_terms * (1.0 / Q), 0.0).astype(jnp.bfloat16)
    returned = jnp.einsum(
        "rq,dre->dqe", plus_table, projected, preferred_element_type=jnp.float32
    ).astype(jnp.bfloat16)
    outgoing = returned.reshape(channels, 1, 1, bond_count, mom_count * mom_local, entries)
    arrived = lax.all_to_all(
        lax.all_to_all(outgoing, "mom", split_axis=4, concat_axis=1, tiled=True),
        "bond",
        split_axis=3,
        concat_axis=2,
        tiled=True,
    )
    arrived = arrived.reshape(channels, mom_count, bond_count, mom_local, row_block, col_block)
    returned_momenta = arrived.transpose(0, 3, 1, 4, 2, 5).reshape(channels, mom_local, NB, NB)
    flowed = vertex.astype(jnp.float32) + product + returned_momenta.astype(jnp.float32)
    return flowed.astype(jnp.bfloat16)


def solution(mesh):
    in_specs = (
        P(None, ("mom", "bond"), None, None),
        P(None, ("mom", "bond"), None, None),
        P(),
        P(),
        P(),
        P(),
        P(),
    )
    out_specs = P(None, ("mom", "bond"), None, None)
    return jax.shard_map(
        per_device, mesh=mesh, in_specs=in_specs, out_specs=out_specs, check_vma=False
    )
```

profile of v0, /device:TPU:1, one launch (start us, length us, event | category | flops | bytes accessed | tf_op | source)
XLA Modules:
  0.0 380.4 jit_solution(17362679247864213683)
XLA Ops:
  0.0 1.4 copy-done
  1.4 5.5 %fusion.59 = (bf16[3,512,512]{2,1,0:T(8,128)(2,1)S(1)}, f32[3,512,512]{2,1,0:T(8,128)}) fusion(bf16[3,1,512,512]{3,2,1,0:T(8,128)(2,1)} %param.7, bf16[3,1,512,512]{3,2,1,0:T(8,128)(2,1)S(1)} %copy-done), kind=kOutput, calls=%fused_computation.101 | convolution fusion | flops 1612185600 | bytes 7864320 | tf_op jit(solution)/shard_map/cqab,cqbd->cqad/dot_general | solution.py:50
  6.9 5.4 %reshape.247 = bf16[3,1,16,32,16,32]{5,4,3,2,0,1:T(8,128)(2,1)} reshape(bf16[3,512,512]{2,1,0:T(8,128)(2,1)S(1)} %get-tuple-element.11) | data formatting | bytes 3145728 | tf_op jit(solution)/shard_map/reshape | solution.py:55
  12.2 7.0 %copy.49 = bf16[3,1,16,32,16,32]{5,3,4,2,0,1:T(8,128)(2,1)} copy(bf16[3,1,16,32,16,32]{5,4,3,2,0,1:T(8,128)(2,1)} %reshape.247) | data formatting | bytes 3145728 | tf_op jit(solution)/shard_map/reshape | solution.py:55
  19.3 8.8 %reshape.248 = bf16[3,16,16,1,1024]{4,2,1,0,3:T(8,128)(2,1)S(1)} reshape(bf16[3,16,16,1,32,32]{5,4,2,1,0,3:T(8,128)(2,1)} %bitcast.92) | data formatting | bytes 3145728 | tf_op jit(solution)/shard_map/reshape | solution.py:58
  28.2 49.6 %all_to_all.54 = bf16[3,16,16,1,1024]{4,2,0,3,1:T(8,128)(2,1)S(1)} all-to-all(bf16[3,16,16,1,1024]{4,2,0,3,1:T(8,128)(2,1)S(1)} %copy.20), channel_id=1, replica_groups=mesh['mom'=16,'bond'=16] {'mom'}, dimensions={1} | all-to-all | bytes 3145728 | tf_op jit(solution)/shard_map/all_to_all | solution.py:57
  77.9 0.9 copy.22
  78.8 29.2 %all_to_all.55 = bf16[3,1,16,16,1024]{4,3,0,1,2:T(8,128)(2,1)S(1)} all-to-all(bf16[3,1,16,16,1024]{4,3,0,1,2:T(8,128)(2,1)S(1)} %copy.22), channel_id=1, replica_groups=mesh['mom'=16,'bond'=16] {'bond'}, dimensions={2} | all-to-all | bytes 3145728 | tf_op jit(solution)/shard_map/all_to_all | solution.py:56
  108.1 0.3 collective-permute-start
  108.4 0.2 copy-done.5
  109.3 72.4 %collective-permute-done = bf16[3,256,1024]{2,1,0:T(8,128)(2,1)} collective-permute-done((bf16[3,256,1024]{2,1,0:T(8,128)(2,1)S(1)}, bf16[3,256,1024]{2,1,0:T(8,128)(2,1)}, u32[]{:S(2)}, u32[]{:S(2)}) %collective-permute-start) | collective-permute-done | bytes 1572896 | tf_op jit(solution)/shard_map/ppermute | solution.py:14
  181.7 1.4 collective-permute-start.1
  183.5 3.3 convolution_bitcast_fusion.1
  186.8 5.3 %copy.27 = f32[3,256,1024]{2,0,1:T(4,128)} copy(f32[3,256,1024]{1,2,0:T(8,128)} %convolution_bitcast_fusion.1) | data formatting | bytes 6291456 | tf_op jit(solution)/shard_map/rq,cqe->cre/transpose | solution.py:81
  192.1 10.4 %fusion.32 = f32[256,1024,3]{1,2,0:T(4,128)} fusion(f32[3,256,1024]{2,0,1:T(4,128)} %copy.27, f32[3,3]{1,0:T(4,128)S(1)} %copy-done.3), kind=kOutput, calls=%fused_computation.58 | convolution fusion | flops 28311552 | bytes 6291492 | tf_op jit(solution)/shard_map/dc,cre->dre/dot_general | solution.py:85
  202.5 16.1 %collective-permute-done.1 = bf16[3,256,1024]{2,1,0:T(8,128)(2,1)S(1)} collective-permute-done((bf16[3,256,1024]{2,1,0:T(8,128)(2,1)}, bf16[3,256,1024]{2,1,0:T(8,128)(2,1)S(1)}, u32[]{:S(2)}, u32[]{:S(2)}) %collective-permute-start.1) | collective-permute-done | bytes 1572896 | tf_op jit(solution)/shard_map/ppermute | solution.py:14
  218.6 2.5 copy.28
  221.2 10.1 %gather_fusion = bf16[1024,3,256]{2,1,0:T(4,128)(2,1)} fusion(bf16[3,256,1024]{1,0,2:T(4,128)(2,1)} %copy.28, s32[1024]{0:T(1024)S(1)} %broadcast_clamp_fusion), kind=kCustom, calls=%fused_computation | custom fusion | bytes 3149824 | tf_op jit(solution)/shard_map/jit(_take)/gather | solution.py:77
  231.3 5.2 %select_bitcast_fusion = bf16[3,256,1024]{1,0,2:T(4,128)(2,1)S(1)} fusion(bf16[1024,3,256]{2,1,0:T(4,128)(2,1)} %gather_fusion, pred[1024]{0:T(1024)(128)(4,1)S(1)} %compare_and_fusion), kind=kLoop, calls=%fused_computation.6 | loop fusion | flops 786432 | bytes 3146752 | tf_op jit(solution)/shard_map/jit(_take)/select_n | solution.py:77
  236.6 3.5 convolution_bitcast_fusion
  240.1 5.3 %copy.31 = f32[3,256,1024]{2,0,1:T(4,128)} copy(f32[3,256,1024]{1,2,0:T(8,128)} %convolution_bitcast_fusion) | data formatting | bytes 6291456 | tf_op jit(solution)/shard_map/rq,cqe->cre/transpose | solution.py:82
  245.3 11.5 %fusion.2 = bf16[3,256,1024]{2,0,1:T(4,128)(2,1)S(1)} fusion(f32[256,1024,3]{1,2,0:T(4,128)} %fusion.32, f32[3,256,1024]{2,0,1:T(4,128)} %copy.31, pred[256,1024]{1,0:T(8,128)(4,1)S(1)} %broadcast_compare_fusion, f32[3,3]{1,0:T(4,128)S(1)} %copy-done.4), kind=kOutput, calls=%fused_computation.11 | convolution fusion | flops 31457280 | bytes 8126500 | tf_op jit(solution)/shard_map/dc,cre->dre/dot_general | solution.py:87
  256.8 3.4 convolution_convert_fusion
  260.2 0.9 copy.33
  261.1 44.3 %all_to_all.56 = bf16[3,1,1,16,16,1024]{5,3,0,2,1,4:T(8,128)(2,1)S(1)} all-to-all(bf16[3,1,1,16,16,1024]{5,3,0,2,1,4:T(8,128)(2,1)S(1)} %copy.33), channel_id=1, replica_groups=mesh['mom'=16,'bond'=16] {'mom'}, dimensions={4} | all-to-all | bytes 3145728 | tf_op jit(solution)/shard_map/all_to_all | solution.py:98
  305.4 0.9 copy.34
  306.3 25.7 %all_to_all.57 = bf16[3,16,1,16,1,1024]{5,1,0,4,2,3:T(8,128)(2,1)S(1)} all-to-all(bf16[3,16,1,16,1,1024]{5,1,0,4,2,3:T(8,128)(2,1)S(1)} %copy.34), channel_id=1, replica_groups=mesh['mom'=16,'bond'=16] {'bond'}, dimensions={3} | all-to-all | bytes 3145728 | tf_op jit(solution)/shard_map/all_to_all | solution.py:97
  332.0 2.6 copy.35
  334.6 9.2 %reshape.254 = f32[3,16,16,1,32,32]{5,4,2,1,0,3:T(8,128)} reshape(f32[3,16,1,16,1,1024]{5,3,1,0,4,2:T(8,128)} %copy.35) | data formatting | bytes 6291456 | tf_op jit(solution)/shard_map/convert_element_type | solution.py:106
  343.8 21.2 %copy.36 = f32[3,1,16,32,16,32]{5,4,3,2,0,1:T(8,128)} copy(f32[3,1,16,32,16,32]{5,3,4,2,0,1:T(8,128)} %bitcast.91) | data formatting | bytes 6291456 | tf_op jit(solution)/shard_map/convert_element_type | solution.py:106
  365.0 10.1 %reshape.253 = f32[3,1,512,512]{3,2,0,1:T(8,128)} reshape(f32[3,1,16,32,16,32]{5,4,3,2,0,1:T(8,128)} %copy.36) | data formatting | bytes 6291456 | tf_op jit(solution)/shard_map/convert_element_type | solution.py:106
  375.1 5.0 %fusion.3 = bf16[3,1,512,512]{3,2,1,0:T(8,128)(2,1)} fusion(f32[3,1,512,512]{3,2,0,1:T(8,128)} %reshape.253, f32[3,512,512]{2,1,0:T(8,128)} %get-tuple-element.12, bf16[3,1,512,512]{3,2,1,0:T(8,128)(2,1)S(1)} %copy-done.2), kind=kLoop, calls=%fused_computation.12 | loop fusion | flops 3145728 | bytes 9437184 | tf_op jit(solution)/shard_map/convert_element_type | solution.py:107
  (33 shorter events, 1.4 us)
Async XLA Ops:
  0.0 1.4 copy-start
  108.0 0.7 copy-start.5
  108.0 0.9 copy-start.6
  108.0 0.9 copy-start.7
  108.1 73.6 %collective-permute-start = (bf16[3,256,1024]{2,1,0:T(8,128)(2,1)S(1)}, bf16[3,256,1024]{2,1,0:T(8,128)(2,1)}, u32[]{:S(2)}, u32[]{:S(2)}) collective-permute-start(bf16[3,256,1024]{2,1,0:T(8,128)(2,1)S(1)} %bitcast.95), channel_id=1, source_target_pairs={{0,128},{16,144},{32,160},{48,176},{64,192},{80,208},{96,224},{112... | collective-permute-start | bytes 4718600 | tf_op jit(solution)/shard_map/ppermute | solution.py:14
  181.7 36.9 %collective-permute-start.1 = (bf16[3,256,1024]{2,1,0:T(8,128)(2,1)}, bf16[3,256,1024]{2,1,0:T(8,128)(2,1)S(1)}, u32[]{:S(2)}, u32[]{:S(2)}) collective-permute-start(bf16[3,256,1024]{2,1,0:T(8,128)(2,1)} %collective-permute-done), channel_id=1, source_target_pairs={{0,8},{1,9},{2,10},{3,11},{4,12},{5,13},{6,14},{7,15},{8,0},{9,1},... | collective-permute-start | bytes 4718600 | tf_op jit(solution)/shard_map/ppermute | solution.py:14
  186.8 5.3 %copy-start.3 = (f32[3,3]{1,0:T(4,128)S(1)}, f32[3,3]{1,0:T(4,128)}, u32[]{:S(2)}) copy-start(f32[3,3]{1,0:T(4,128)} %param.9) | copy-start | bytes 112
  240.1 5.3 %copy-start.4 = (f32[3,3]{1,0:T(4,128)S(1)}, f32[3,3]{1,0:T(4,128)}, u32[]{:S(2)}) copy-start(f32[3,3]{1,0:T(4,128)} %param.10) | copy-start | bytes 112
  365.0 10.1 %copy-start.2 = (bf16[3,1,512,512]{3,2,1,0:T(8,128)(2,1)S(1)}, bf16[3,1,512,512]{3,2,1,0:T(8,128)(2,1)}, u32[]{:S(2)}) copy-start(bf16[3,1,512,512]{3,2,1,0:T(8,128)(2,1)} %param.7) | copy-start | bytes 4718596
  375.1 5.0 %copy-start.1 = (bf16[3,1,512,512]{3,2,1,0:T(8,128)(2,1)S(1)}, bf16[3,1,512,512]{3,2,1,0:T(8,128)(2,1)}, u32[]{:S(2)}) copy-start(bf16[3,1,512,512]{3,2,1,0:T(8,128)(2,1)} %param.8) | copy-start | bytes 4718596
where the time goes:
time: 387 us; the launch traced here: 380 us
  blocking collectives  149 us (39%)
  local copies, waits for them, and re-layouts  92.6 us (24%)
  waiting for transfers between devices  88.6 us (23%)
  matrix products  37.5 us (10%)
  other arithmetic  10.8 us (3%)
    ppermute x2, waiting for transfers between devices, from_partner(): lax.ppermute(x, axis, [(i, i ^ 1 << bit) for i in range(lax.axis_size(axi...  88.6 us
    all_to_all x1, blocking collectives, per_device(): lax.all_to_all(shaped.transpose(0, 2, 4, 1, 3, 5).reshape(depth_count, mo...  49.6 us
    all_to_all x1, blocking collectives, per_device(): lax.all_to_all(outgoing, 'mom', split_axis=4, concat_axis=1, tiled=True)  44.3 us
    convert_element_type x4, local copies, waits for them, and re-layouts, per_device(): returned_momenta.astype(jnp.float32)  43 us
    all_to_all x1, blocking collectives, per_device(): lax.all_to_all(lax.all_to_all(shaped.transpose(0, 2, 4, 1, 3, 5).reshape(...  29.2 us
    all_to_all x1, blocking collectives, per_device(): lax.all_to_all(lax.all_to_all(outgoing, 'mom', split_axis=4, concat_axis=...  25.7 us
    reshape x2, local copies, waits for them, and re-layouts, per_device(): rounded.reshape(depth_count, mom_local, mom_count, row_block, bond_count,...  12.4 us
    dot_general x1, matrix products, per_device(): jnp.einsum('dc,cre->dre', cross_mix, cross_lattice, precision=lax.Precisi...  11.5 us
  transfers between devices with their start and end apart: 2, of which 2 were waited for; matrix products, arithmetic and copies ran while one was open for 5% of the time, Pallas kernels for 0%

commit v1 on v0

v1 whole, which is shorter than its diff:
```python
import math

import jax
import jax.numpy as jnp
from jax import lax
from jax.experimental import pallas as pl
from jax.experimental.pallas import tpu as pltpu
from jax.sharding import PartitionSpec as P

G = 16
NB = 512
Q = 256
NCH = 3
HALF = NB // 2
SUB = 8
LANES = 128
TILE_COLS = NB // LANES
PAIR = SUB // 2
AXES = ("mom", "bond")

CAS = [math.cos(2 * math.pi * n / G) + math.sin(2 * math.pi * n / G) for n in range(8)]
CAS[6] = 0.0


def iota(shape, dim):
    return lax.broadcasted_iota(jnp.int32, shape, dim)


def orbit_select(partner_row):
    row = iota((NB, NB), 0)
    bond = (row // SUB) * PAIR + row % PAIR
    source = jnp.where(row % SUB < PAIR, iota((NB, NB), 1), partner_row)
    return (source == bond).astype(jnp.float32)


def partner_matrix(partner_row):
    return (partner_row == iota((NB, NB), 0)).astype(jnp.float32)


def dot(a, b):
    return jnp.dot(a, b, preferred_element_type=jnp.float32)


def product_kernel(vertex_ref, loop_ref, partner_ref, sent_ref, sum_ref, swap_ref, select_ref):
    @pl.when(pl.program_id(0) == 0)
    def _():
        partner_row = partner_ref[...]
        swap_ref[...] = partner_matrix(partner_row).astype(jnp.bfloat16)
        select_ref[...] = orbit_select(partner_row).astype(jnp.bfloat16)

    vertex = vertex_ref[0, 0]
    half_product = dot(vertex, loop_ref[0, 0]).astype(jnp.bfloat16)
    product = dot(half_product, vertex)
    sum_ref[0] = vertex.astype(jnp.float32) + product
    rounded = product.astype(jnp.bfloat16)
    lower = dot(rounded[HALF:], swap_ref[...]).astype(jnp.bfloat16)
    ordered = dot(select_ref[...], jnp.concatenate([rounded[:HALF], lower], axis=0))
    for j in range(TILE_COLS):
        piece = ordered[:, j * LANES : (j + 1) * LANES].reshape(NB // SUB, SUB, LANES)
        sent_ref[:, j, 0] = piece.astype(jnp.bfloat16)


def cas_values(phase):
    low = phase & 7
    value = jnp.full(phase.shape, CAS[0], jnp.float32)
    for n in range(1, 8):
        value = jnp.where(low == n, CAS[n], value)
    return jnp.where(phase & 8 != 0, -value, value)


def lattice_kernel(
    place_ref, own_mix_ref, cross_mix_ref, shells_s, partner_s, arrived_ref, grid_ref, shells_ref, partner_ref,
    back_ref, in_ref, out_ref,
):
    place = place_ref[0]
    tile_row = place // TILE_COLS
    tile_col = place % TILE_COLS
    shape = (Q, Q)
    point = grid_ref[...]
    disp = iota(shape, 0)
    phase = (disp // G) * (point // G) + (disp % G) * (point % G)
    plus = cas_values(phase & 15)
    minus = cas_values((-phase) & 15)
    plus_back = plus.T.astype(jnp.bfloat16)
    tables = jnp.concatenate([plus, minus], axis=0).astype(jnp.bfloat16)

    shell_row = shells_ref[pl.ds(tile_col, 1), :]
    pick = (iota((NB, LANES), 0) == partner_ref[pl.ds(tile_col, 1), :]).astype(jnp.float32).astype(jnp.bfloat16)
    crossed_row = jnp.zeros((SUB, LANES), jnp.float32)
    for j in range(TILE_COLS):
        part = jnp.broadcast_to(shells_ref[pl.ds(j, 1), :], (SUB, LANES)).astype(jnp.float32).astype(jnp.bfloat16)
        crossed_row += dot(part, pick[j * LANES : (j + 1) * LANES])
    crossed_shell_row = crossed_row[:1].astype(jnp.int32)
    lattice_point = iota((Q, LANES), 0)
    centre_x = (lattice_point // G + G // 2) % G - G // 2
    centre_y = (lattice_point % G + G // 2) % G - G // 2
    cycle = jnp.maximum(jnp.abs(centre_x), jnp.abs(centre_y))

    for c in range(NCH):
        in_ref[c] = arrived_ref[:, c].astype(jnp.float32).reshape(Q * SUB, LANES)
    for s in range(PAIR):
        bond = tile_row * PAIR + s
        own_keep = cycle <= shell_row + shells_s[bond]
        cross_keep = cycle <= crossed_shell_row + shells_s[partner_s[bond]]
        lattice = []
        for c in range(NCH):
            own = in_ref[c, pl.ds(s, Q, stride=SUB), :].astype(jnp.bfloat16)
            crossed = in_ref[c, pl.ds(s + PAIR, Q, stride=SUB), :].astype(jnp.bfloat16)
            lattice.append(dot(tables, jnp.concatenate([own, crossed], axis=1)))
        for d in range(NCH):
            own_sum = jnp.zeros((Q, LANES), jnp.float32)
            cross_sum = jnp.zeros((Q, LANES), jnp.float32)
            for c in range(NCH):
                own_gain = own_mix_ref[d, c] * (1.0 / Q)
                cross_gain = cross_mix_ref[d, c] * (1.0 / Q)
                own_sum += own_gain * lattice[c][:Q, :LANES] + cross_gain * lattice[c][Q:, LANES:]
                cross_sum += own_gain * lattice[c][:Q, LANES:] + cross_gain * lattice[c][Q:, :LANES]
            projected = jnp.concatenate(
                [jnp.where(own_keep, own_sum, 0.0), jnp.where(cross_keep, cross_sum, 0.0)], axis=1
            ).astype(jnp.bfloat16)
            returned = dot(plus_back, projected)
            out_ref[d, pl.ds(s, Q, stride=SUB), :] = returned[:, :LANES]
            out_ref[d, pl.ds(s + PAIR, Q, stride=SUB), :] = returned[:, LANES:]
    for d in range(NCH):
        back_ref[:, d] = out_ref[d].reshape(Q, SUB, LANES).astype(jnp.bfloat16)


def flow_kernel(back_ref, sum_ref, partner_ref, flowed_ref, swap_ref, select_ref):
    @pl.when(pl.program_id(0) == 0)
    def _():
        partner_row = partner_ref[...]
        swap_ref[...] = partner_matrix(partner_row).astype(jnp.bfloat16)
        select_ref[...] = orbit_select(partner_row).T.astype(jnp.bfloat16)

    columns = [
        back_ref[:, j, 0].astype(jnp.float32).reshape(NB, LANES).astype(jnp.bfloat16) for j in range(TILE_COLS)
    ]
    returned = dot(select_ref[...], jnp.concatenate(columns, axis=1))
    lower = dot(returned[HALF:].astype(jnp.bfloat16), swap_ref[...])
    flowed_ref[0, 0, :HALF] = (sum_ref[0, :HALF] + returned[:HALF]).astype(jnp.bfloat16)
    flowed_ref[0, 0, HALF:] = (sum_ref[0, HALF:] + lower).astype(jnp.bfloat16)


def per_device(vertex, loop_matrix, own_mix, cross_mix, shells, partner, grid_index):
    f32, bf16 = jnp.float32, jnp.bfloat16
    tiles = (NB // SUB, TILE_COLS, NCH, SUB, LANES)
    matrix_spec = pl.BlockSpec((1, 1, NB, NB), lambda c: (c, 0, 0, 0))
    tiles_spec = pl.BlockSpec((NB // SUB, TILE_COLS, 1, SUB, LANES), lambda c: (0, 0, c, 0, 0))
    sum_spec = pl.BlockSpec((1, NB, NB), lambda c: (c, 0, 0))
    partner_spec = pl.BlockSpec((1, NB), lambda c: (0, 0))
    selectors = [pltpu.VMEM((NB, NB), bf16), pltpu.VMEM((NB, NB), bf16)]
    params = pltpu.CompilerParams(vmem_limit_bytes=40 << 20)
    partner_row = partner.reshape(1, NB)
    sent, vertex_sum = pl.pallas_call(
        product_kernel,
        grid=(NCH,),
        in_specs=[matrix_spec, matrix_spec, partner_spec],
        out_specs=[tiles_spec, sum_spec],
        out_shape=[jax.ShapeDtypeStruct(tiles, bf16), jax.ShapeDtypeStruct((NCH, NB, NB), f32)],
        scratch_shapes=selectors,
        compiler_params=params,
        name="product",
    )(vertex, loop_matrix, partner_row)
    arrived = lax.all_to_all(sent.reshape(Q, NCH, SUB, LANES), AXES, 0, 0, tiled=True)
    place = lax.axis_index(AXES).astype(jnp.int32).reshape(1)
    smem = pl.BlockSpec(memory_space=pltpu.SMEM)
    vmem = pl.BlockSpec(memory_space=pltpu.VMEM)
    back = pl.pallas_call(
        lattice_kernel,
        in_specs=[smem] * 5 + [vmem] * 4,
        out_specs=vmem,
        out_shape=jax.ShapeDtypeStruct((Q, NCH, SUB, LANES), bf16),
        scratch_shapes=[pltpu.VMEM((NCH, Q * SUB, LANES), f32), pltpu.VMEM((NCH, Q * SUB, LANES), f32)],
        compiler_params=params,
        name="lattice",
    )(
        place, own_mix, cross_mix, shells, partner, arrived,
        grid_index.reshape(1, Q), shells.reshape(TILE_COLS, LANES), partner.reshape(TILE_COLS, LANES),
    )
    received = lax.all_to_all(back, AXES, 0, 0, tiled=True).reshape(tiles)
    return pl.pallas_call(
        flow_kernel,
        grid=(NCH,),
        in_specs=[tiles_spec, sum_spec, partner_spec],
        out_specs=matrix_spec,
        out_shape=jax.ShapeDtypeStruct((NCH, 1, NB, NB), bf16),
        scratch_shapes=selectors,
        compiler_params=params,
        name="flow",
    )(received, vertex_sum, partner_row)


def solution(mesh):
    split = P(None, ("mom", "bond"), None, None)
    return jax.shard_map(
        per_device, mesh=mesh, in_specs=(split, split, P(), P(), P(), P(), P()), out_specs=split, check_vma=False
    )
```

time: 387 us -> 123 us (0.32); the launches traced: 380 us -> 123 us
  blocking collectives: 149 us -> 48.4 us
  local copies, waits for them, and re-layouts: 92.6 us -> 5.14 us
  waiting for transfers between devices: 88.6 us -> 41.1 us
  matrix products: 37.5 us -> 0 us
  starting transfers between devices: 1.65 us -> 15.7 us
  Pallas kernels: 0 us -> 12.6 us
  other arithmetic: 10.8 us -> 0 us
    all_to_all x4 -> x1, blocking collectives: 149 us -> 48.4 us  [per_device(): received = lax.all_to_all(back, AXES, 0, 0, tiled=True).reshape(tiles)]
    ppermute x2 -> x0, waiting for transfers between devices: 88.6 us -> none  [from_partner(): lax.ppermute(x, axis, [(i, i ^ 1 << bit) for i in range(lax.axis_size(axi...]
    convert_element_type x4 -> x0, local copies, waits for them, and re-layouts: 43 us -> none  [per_device(): returned_momenta.astype(jnp.float32)]
    all_to_all x0 -> x1, waiting for transfers between devices: none -> 41.1 us  [per_device(): lax.all_to_all(sent.reshape(Q, NCH, SUB, LANES), AXES, 0, 0, tiled=True)]
    dot_general x6 -> x0, matrix products: 37.5 us -> none  [the longest x1 11.5 us: per_device(): jnp.einsum('dc,cre->dre', cross_mix, cross_lattice, precision=lax.Precisi...]
    reshape x7 -> x0, local copies, waits for them, and re-layouts: 22.3 us -> none  [the longest x2 12.4 us: per_device(): rounded.reshape(depth_count, mom_local, mom_count, row_block, bond_count,...]
    all_to_all x0 -> x1, starting transfers between devices: none -> 15.7 us  [per_device(): lax.all_to_all(sent.reshape(Q, NCH, SUB, LANES), AXES, 0, 0, tiled=True)]
    pallas_call x0 -> x3, Pallas kernels: none -> 12.6 us  [the longest x1 4.69 us: per_device(): pl.pallas_call(product_kernel, grid=(NCH,), in_specs=[matrix_spec, matrix...]
  transfers between devices with their start and end apart: 2 -> 1, of which waited for: 2 -> 1; matrix products, arithmetic and copies ran while one was open for 5% -> 0% of each run, Pallas kernels for 0% -> 0%
where the time goes in v1:
time: 123 us
  blocking collectives  48.4 us (39%)
  waiting for transfers between devices  41.1 us (33%)
  starting transfers between devices  15.7 us (13%)
  Pallas kernels  12.6 us (10%)
  local copies, waits for them, and re-layouts  5.14 us (4%)
    all_to_all x1, blocking collectives, per_device(): received = lax.all_to_all(back, AXES, 0, 0, tiled=True).reshape(tiles)  48.4 us
    all_to_all x1, waiting for transfers between devices, per_device(): lax.all_to_all(sent.reshape(Q, NCH, SUB, LANES), AXES, 0, 0, tiled=True)  41.1 us
    all_to_all x1, starting transfers between devices, per_device(): lax.all_to_all(sent.reshape(Q, NCH, SUB, LANES), AXES, 0, 0, tiled=True)  15.7 us
    unnamed x20, local copies, waits for them, and re-layouts  5.14 us
    pallas_call x1, Pallas kernels, per_device(): pl.pallas_call(product_kernel, grid=(NCH,), in_specs=[matrix_spec, matrix...  4.69 us
    pallas_call x1, Pallas kernels, per_device(): pl.pallas_call(lattice_kernel, in_specs=[smem] * 5 + [vmem] * 4, out_spec...  4.48 us
    pallas_call x1, Pallas kernels, per_device(): pl.pallas_call(flow_kernel, grid=(NCH,), in_specs=[tiles_spec, sum_spec,...  3.45 us
  transfers between devices with their start and end apart: 1, of which 1 were waited for; matrix products, arithmetic and copies ran while one was open for 0% of the time, Pallas kernels for 0%

profile of v1, /device:TPU:1, one launch (start us, length us, event | category | flops | bytes accessed | tf_op | source)
XLA Modules:
  0.0 123.0 jit_solution(11683478949436927009)
XLA Ops:
  0.0 0.0 copy-start.2
  0.0 1.4 %copy-done.2 = bf16[3,1,512,512]{3,2,1,0:T(8,128)(2,1)S(1)} copy-done((bf16[3,1,512,512]{3,2,1,0:T(8,128)(2,1)S(1)}, bf16[3,1,512,512]{3,2,1,0:T(8,128)(2,1)}, u32[]{:S(2)}) %copy-start.2) | copy-done | bytes 1572888
  1.4 0.0 copy-start.3
  1.4 1.4 %copy-done.3 = bf16[3,1,512,512]{3,2,1,0:T(8,128)(2,1)S(1)} copy-done((bf16[3,1,512,512]{3,2,1,0:T(8,128)(2,1)S(1)}, bf16[3,1,512,512]{3,2,1,0:T(8,128)(2,1)}, u32[]{:S(2)}) %copy-start.3) | copy-done | bytes 1572888
  2.8 0.0 copy-start.4
  2.8 0.7 copy-done.4
  3.5 4.7 %product.1 = (bf16[64,4,3,8,128]{4,3,2,1,0:T(8,128)(2,1)}, f32[3,512,512]{2,1,0:T(8,128)S(1)}) custom-call(bf16[3,1,512,512]{3,2,1,0:T(8,128)(2,1)S(1)} %copy-done.2, bf16[3,1,512,512]{3,2,1,0:T(8,128)(2,1)S(1)} %copy-done.3, s32[1,512]{1,0:T(1,128)S(1)} %bitcast.8), custom_call_target="tpu_custom_call" | custom-call | tf_op jit(solution)/shard_map/product/pallas_call | solution.py:154
  8.2 0.0 copy-start
  8.2 1.6 %copy-done = f32[3,512,512]{2,1,0:T(8,128)} copy-done((f32[3,512,512]{2,1,0:T(8,128)}, f32[3,512,512]{2,1,0:T(8,128)S(1)}, u32[]{:S(2)}) %copy-start) | copy-done | bytes 3145752
  9.8 0.0 copy-start.5
  9.8 0.0 copy-start.6
  9.8 0.0 copy-start.7
  9.8 0.0 copy-start.8
  9.8 0.0 copy-start.9
  9.8 15.7 %all-to-all-start = ((bf16[256,3,8,128]{3,2,1,0:T(8,128)(2,1)}), bf16[256,3,8,128]{3,2,1,0:T(8,128)(2,1)S(1)}, u32[]{:S(2)}, u32[]{:S(2)}) async-start(bf16[256,3,8,128]{3,2,1,0:T(8,128)(2,1)} %bitcast.2), calls=%async_computation | async-start | bytes 3145728 | tf_op jit(solution)/shard_map/all_to_all | solution.py:164
  25.5 41.1 %all-to-all-done.arrived_ref = bf16[256,3,8,128]{3,2,1,0:T(8,128)(2,1)S(1)} async-done(((bf16[256,3,8,128]{3,2,1,0:T(8,128)(2,1)}), bf16[256,3,8,128]{3,2,1,0:T(8,128)(2,1)S(1)}, u32[]{:S(2)}, u32[]{:S(2)}) %all-to-all-start) | async-done | bytes 1572896 | tf_op jit(solution)/shard_map/all_to_all | solution.py:164
  66.6 0.0 copy-done.5
  66.6 0.0 copy-done.6
  66.6 0.0 copy-done.7
  66.6 0.0 copy-done.8
  66.6 0.0 copy-done.9
  66.7 4.5 %lattice.1 = bf16[256,3,8,128]{3,2,1,0:T(8,128)(2,1)S(1)} custom-call(s32[1]{0:T(128)} %bitcast.place_ref, f32[3,3]{1,0:T(4,128)S(1)} %copy-done.7, f32[3,3]{1,0:T(4,128)S(1)} %copy-done.8, s32[512]{0:T(512)S(1)} %copy-done.6, s32[512]{0:T(512)S(1)} %copy-done.5, bf16[256,3,8,128]{3,2,1,0:T(8,128)(2,1)S(1)} %all-to-all-done.arrived_ref, ...), custom_call_target="tpu_custom_call" | custom-call | tf_op jit(solution)/shard_map/lattice/pallas_call | solution.py:168
  71.1 0.0 copy-start.1
  71.1 48.4 %all_to_all.10 = bf16[256,3,8,128]{3,2,1,0:T(8,128)(2,1)S(1)} all-to-all(bf16[256,3,8,128]{3,2,1,0:T(8,128)(2,1)S(1)} %lattice.1), channel_id=1, replica_groups=mesh['mom'=16,'bond'=16] {'mom','bond'}, dimensions={0} | all-to-all | bytes 3145728 | tf_op jit(solution)/shard_map/all_to_all | solution.py:180
  119.5 0.0 copy-done.1
  119.5 3.5 %flow.1 = bf16[3,1,512,512]{3,2,1,0:T(8,128)(2,1)} custom-call(bf16[64,4,3,8,128]{4,3,2,1,0:T(8,128)(2,1)S(1)} %bitcast.7, f32[3,512,512]{2,1,0:T(8,128)S(1)} %copy-done.1, s32[1,512]{1,0:T(1,128)S(1)} %bitcast.10), custom_call_target="tpu_custom_call" | custom-call | tf_op jit(solution)/shard_map/flow/pallas_call | solution.py:181
Async XLA Ops:
  0.0 1.4 %copy-start.2 = (bf16[3,1,512,512]{3,2,1,0:T(8,128)(2,1)S(1)}, bf16[3,1,512,512]{3,2,1,0:T(8,128)(2,1)}, u32[]{:S(2)}) copy-start(bf16[3,1,512,512]{3,2,1,0:T(8,128)(2,1)} %vertex_ref.1) | copy-start | bytes 4718596
  1.4 1.4 %copy-start.3 = (bf16[3,1,512,512]{3,2,1,0:T(8,128)(2,1)S(1)}, bf16[3,1,512,512]{3,2,1,0:T(8,128)(2,1)}, u32[]{:S(2)}) copy-start(bf16[3,1,512,512]{3,2,1,0:T(8,128)(2,1)} %loop_ref.1) | copy-start | bytes 4718596
  2.8 0.7 copy-start.4
  8.2 1.6 %copy-start = (f32[3,512,512]{2,1,0:T(8,128)}, f32[3,512,512]{2,1,0:T(8,128)S(1)}, u32[]{:S(2)}) copy-start(f32[3,512,512]{2,1,0:T(8,128)S(1)} %get-tuple-element.8.sum_ref) | copy-start | bytes 9437188
  9.8 56.8 %copy-start.5 = (s32[512]{0:T(512)S(1)}, s32[512]{0:T(512)}, u32[]{:S(2)}) copy-start(s32[512]{0:T(512)} %partner_s.1) | copy-start | bytes 6148
  9.8 56.8 %copy-start.6 = (s32[512]{0:T(512)S(1)}, s32[512]{0:T(512)}, u32[]{:S(2)}) copy-start(s32[512]{0:T(512)} %shells_s.1) | copy-start | bytes 6148
  9.8 56.8 %copy-start.7 = (f32[3,3]{1,0:T(4,128)S(1)}, f32[3,3]{1,0:T(4,128)}, u32[]{:S(2)}) copy-start(f32[3,3]{1,0:T(4,128)} %own_mix_ref.1) | copy-start | bytes 112
  9.8 56.8 %copy-start.8 = (f32[3,3]{1,0:T(4,128)S(1)}, f32[3,3]{1,0:T(4,128)}, u32[]{:S(2)}) copy-start(f32[3,3]{1,0:T(4,128)} %cross_mix_ref.1) | copy-start | bytes 112
  9.8 56.8 %copy-start.9 = (s32[256]{0:T(256)S(1)}, s32[256]{0:T(256)}, u32[]{:S(2)}) copy-start(s32[256]{0:T(256)} %param.13) | copy-start | bytes 3076
  9.8 56.8 %all-to-all-start = ((bf16[256,3,8,128]{3,2,1,0:T(8,128)(2,1)}), bf16[256,3,8,128]{3,2,1,0:T(8,128)(2,1)S(1)}, u32[]{:S(2)}, u32[]{:S(2)}) async-start(bf16[256,3,8,128]{3,2,1,0:T(8,128)(2,1)} %bitcast.2), calls=%async_computation | async-start | bytes 3145728 | tf_op jit(solution)/shard_map/all_to_all | solution.py:164
  71.1 48.4 %copy-start.1 = (f32[3,512,512]{2,1,0:T(8,128)S(1)}, f32[3,512,512]{2,1,0:T(8,128)}, u32[]{:S(2)}) copy-start(f32[3,512,512]{2,1,0:T(8,128)} %copy-done) | copy-start | bytes 9437188

commit v2 on v1

v2 whole, which is shorter than its diff:
```python
import math

import jax
import jax.numpy as jnp
from jax import lax
from jax.experimental import pallas as pl
from jax.experimental.pallas import tpu as pltpu
from jax.sharding import PartitionSpec as P

G = 16
NB = 512
Q = 256
NCH = 3
HALF = NB // 2
SUB = 8
LANES = 128
TILE_COLS = NB // LANES
PAIR = SUB // 2
TILES = (HALF // SUB, 2, TILE_COLS, NCH, SUB, LANES)
AXES = ("mom", "bond")

CAS = [math.cos(2 * math.pi * n / G) + math.sin(2 * math.pi * n / G) for n in range(8)]
CAS[6] = 0.0

SMEM = pl.BlockSpec(memory_space=pltpu.SMEM)
VMEM = pl.BlockSpec(memory_space=pltpu.VMEM)
HBM = pl.BlockSpec(memory_space=pltpu.HBM)
FULL = pltpu.CompilerParams(vmem_limit_bytes=63 << 20)
PARAMS = pltpu.CompilerParams(vmem_limit_bytes=40 << 20)


def iota(shape, dim):
    return lax.broadcasted_iota(jnp.int32, shape, dim)


def to_bf16(flags):
    return flags.astype(jnp.float32).astype(jnp.bfloat16)


def dot(a, b):
    return jnp.dot(a, b, preferred_element_type=jnp.float32)


def partner_blocks(partner_ref):
    rows = iota((HALF, HALF), 0)
    upper_of = to_bf16(partner_ref[:, HALF:] == rows)
    lower_of = to_bf16(partner_ref[:, :HALF] == rows + HALF)
    return upper_of, lower_of


def swap_columns(x, upper_of, lower_of):
    x = x.astype(jnp.bfloat16)
    return jnp.concatenate([dot(x[:, HALF:], lower_of), dot(x[:, :HALF], upper_of)], axis=1)


def interleave(first, second):
    low = iota(first.shape, 1) < PAIR
    even = jnp.where(low, first, pltpu.roll(second, PAIR, 1))
    odd = jnp.where(low, pltpu.roll(first, PAIR, 1), second)
    return even, odd


def by_groups(x):
    return x.reshape(HALF // SUB, SUB, NB)


def product_of(vertex, loop):
    return dot(dot(vertex, loop).astype(jnp.bfloat16), vertex)


def fetch(pairs, sems):
    copies = [
        [pltpu.make_async_copy(source.at[c, 0], target.at[c], sems.at[i, c]) for i, (source, target) in enumerate(pairs)]
        for c in range(NCH)
    ]
    for group in copies:
        for copy in group:
            copy.start()
    return copies


def product_kernel(vertex_hbm, loop_hbm, partner_ref, sent_hbm, vertex_buf, loop_buf, sems, sent_ref, sent_sems):
    copies = fetch([(vertex_hbm, vertex_buf), (loop_hbm, loop_buf)], sems)
    upper_of, lower_of = partner_blocks(partner_ref)
    sends = []
    for c in range(NCH):
        for copy in copies[c]:
            copy.wait()
        product = product_of(vertex_buf[c], loop_buf[c])
        swapped = swap_columns(product[HALF:], upper_of, lower_of).astype(jnp.bfloat16)
        crossed = dot(upper_of, swapped)
        for half, rows in enumerate(interleave(by_groups(product[:HALF]), by_groups(crossed))):
            for j in range(TILE_COLS):
                sent_ref[:, half, j, c] = rows[:, :, j * LANES : (j + 1) * LANES].astype(jnp.bfloat16)
        sends.append(pltpu.make_async_copy(sent_ref.at[:, :, :, c], sent_hbm.at[:, :, :, c], sent_sems.at[c]))
        sends[c].start()
    for copy in sends:
        copy.wait()


def cas_values(phase):
    low = phase & 7
    value = jnp.full(phase.shape, CAS[0], jnp.float32)
    for n in range(1, 8):
        value = jnp.where(low == n, CAS[n], value)
    return jnp.where(phase & 8 != 0, -value, value)


def side_kernel(
    tile_col_ref, vertex_hbm, loop_hbm, grid_ref, shells_ref, partner_ref, sum_ref, tables_ref, back_ref, shell_rows_ref,
    vertex_buf, loop_buf, sems,
):
    copies = fetch([(vertex_hbm, vertex_buf), (loop_hbm, loop_buf)], sems)
    point = grid_ref[...]
    disp = iota((Q, Q), 0)
    phase = (disp // G) * (point // G) + (disp % G) * (point % G)
    plus = cas_values(phase & 15)
    tables_ref[:Q] = plus.astype(jnp.bfloat16)
    tables_ref[Q:] = cas_values((-phase) & 15).astype(jnp.bfloat16)
    back_ref[...] = plus.T.astype(jnp.bfloat16)
    tile_col = tile_col_ref[0]
    pick = to_bf16(iota((NB, LANES), 0) == partner_ref[pl.ds(tile_col, 1), :])
    crossed_row = jnp.zeros((SUB, LANES), jnp.float32)
    for j in range(TILE_COLS):
        part = to_bf16(jnp.broadcast_to(shells_ref[pl.ds(j, 1), :], (SUB, LANES)))
        crossed_row += dot(part, pick[j * LANES : (j + 1) * LANES])
    own_row = jnp.broadcast_to(shells_ref[pl.ds(tile_col, 1), :], (SUB, LANES))
    shell_rows_ref[...] = jnp.where(iota((SUB, LANES), 0) < PAIR, own_row, crossed_row.astype(jnp.int32))
    for c in range(NCH):
        for copy in copies[c]:
            copy.wait()
        vertex = vertex_buf[c]
        sum_ref[c] = vertex.astype(jnp.float32) + product_of(vertex, loop_buf[c])


def lattice_kernel(
    tile_row_ref, own_mix_ref, cross_mix_ref, shells_s, partner_s, arrived_ref, tables_ref, plus_back_ref,
    shell_rows_ref, back_ref, in_ref, out_ref,
):
    tile_row = tile_row_ref[0]
    lattice_point = iota((Q, LANES), 0)
    centre_x = (lattice_point // G + G // 2) % G - G // 2
    centre_y = (lattice_point % G + G // 2) % G - G // 2
    cycle = jnp.maximum(jnp.abs(centre_x), jnp.abs(centre_y))
    for c in range(NCH):
        in_ref[c] = arrived_ref[:, c].astype(jnp.float32).reshape(Q * SUB, LANES)
    for s in range(PAIR):
        bond = tile_row * PAIR + s
        own_keep = cycle <= shell_rows_ref[0:1, :] + shells_s[bond]
        cross_keep = cycle <= shell_rows_ref[PAIR : PAIR + 1, :] + shells_s[partner_s[bond]]
        lattice = []
        for c in range(NCH):
            own = in_ref[c, pl.ds(s, Q, stride=SUB), :].astype(jnp.bfloat16)
            crossed = in_ref[c, pl.ds(s + PAIR, Q, stride=SUB), :].astype(jnp.bfloat16)
            lattice.append(dot(tables_ref[...], jnp.concatenate([own, crossed], axis=1)))
        for d in range(NCH):
            own_sum = jnp.zeros((Q, LANES), jnp.float32)
            cross_sum = jnp.zeros((Q, LANES), jnp.float32)
            for c in range(NCH):
                own_gain = own_mix_ref[d, c] * (1.0 / Q)
                cross_gain = cross_mix_ref[d, c] * (1.0 / Q)
                own_sum += own_gain * lattice[c][:Q, :LANES] + cross_gain * lattice[c][Q:, LANES:]
                cross_sum += own_gain * lattice[c][:Q, LANES:] + cross_gain * lattice[c][Q:, :LANES]
            projected = jnp.concatenate(
                [jnp.where(own_keep, own_sum, 0.0), jnp.where(cross_keep, cross_sum, 0.0)], axis=1
            ).astype(jnp.bfloat16)
            returned = dot(plus_back_ref[...], projected)
            out_ref[d, pl.ds(s, Q, stride=SUB), :] = returned[:, :LANES]
            out_ref[d, pl.ds(s + PAIR, Q, stride=SUB), :] = returned[:, LANES:]
    for d in range(NCH):
        back_ref[:, d] = out_ref[d].reshape(Q, SUB, LANES).astype(jnp.bfloat16)


def flow_kernel(received_ref, sum_ref, partner_ref, flowed_hbm, flowed_buf, sems):
    upper_of, lower_of = partner_blocks(partner_ref)
    copies = []
    for c in range(NCH):
        halves = [
            jnp.concatenate([received_ref[:, half, j, c].astype(jnp.float32) for j in range(TILE_COLS)], axis=2)
            for half in range(2)
        ]
        own, crossed = interleave(*halves)
        rows = dot(lower_of, crossed.reshape(HALF, NB).astype(jnp.bfloat16))
        lower = swap_columns(rows, upper_of, lower_of)
        flowed_buf[c, :HALF] = (sum_ref[c, :HALF] + own.reshape(HALF, NB)).astype(jnp.bfloat16)
        flowed_buf[c, HALF:] = (sum_ref[c, HALF:] + lower).astype(jnp.bfloat16)
        copies.append(pltpu.make_async_copy(flowed_buf.at[c], flowed_hbm.at[c, 0], sems.at[c]))
        copies[c].start()
    for copy in copies:
        copy.wait()


def per_device(vertex, loop_matrix, own_mix, cross_mix, shells, partner, grid_index):
    f32, bf16, i32 = jnp.float32, jnp.bfloat16, jnp.int32
    shape = jax.ShapeDtypeStruct
    fetched = [
        pltpu.VMEM((NCH, NB, NB), bf16),
        pltpu.VMEM((NCH, NB, NB), bf16),
        pltpu.SemaphoreType.DMA((2, NCH)),
    ]
    partner_row = partner.reshape(1, NB)
    place = lax.axis_index(AXES).astype(i32)
    sent = pl.pallas_call(
        product_kernel,
        in_specs=[HBM, HBM, VMEM],
        out_specs=HBM,
        out_shape=shape(TILES, bf16),
        scratch_shapes=[*fetched, pltpu.VMEM(TILES, bf16), pltpu.SemaphoreType.DMA((NCH,))],
        compiler_params=FULL,
        name="product",
    )(vertex, loop_matrix, partner_row)
    arrived = lax.all_to_all(sent.reshape(Q, NCH, SUB, LANES), AXES, 0, 0, tiled=True)
    vertex_sum, tables, plus_back, shell_rows = pl.pallas_call(
        side_kernel,
        in_specs=[SMEM, HBM, HBM, VMEM, VMEM, VMEM],
        out_specs=[VMEM] * 4,
        out_shape=[shape((NCH, NB, NB), f32), shape((2 * Q, Q), bf16), shape((Q, Q), bf16), shape((SUB, LANES), i32)],
        scratch_shapes=fetched,
        compiler_params=PARAMS,
        name="side",
    )(
        (place % TILE_COLS).reshape(1), vertex, loop_matrix, grid_index.reshape(1, Q),
        shells.reshape(TILE_COLS, LANES), partner.reshape(TILE_COLS, LANES),
    )
    back = pl.pallas_call(
        lattice_kernel,
        in_specs=[SMEM] * 5 + [VMEM] * 4,
        out_specs=VMEM,
        out_shape=shape((Q, NCH, SUB, LANES), bf16),
        scratch_shapes=[pltpu.VMEM((NCH, Q * SUB, LANES), f32), pltpu.VMEM((NCH, Q * SUB, LANES), f32)],
        compiler_params=PARAMS,
        name="lattice",
    )((place // TILE_COLS).reshape(1), own_mix, cross_mix, shells, partner, arrived, tables, plus_back, shell_rows)
    received = lax.all_to_all(back, AXES, 0, 0, tiled=True).reshape(TILES)
    return pl.pallas_call(
        flow_kernel,
        in_specs=[VMEM, VMEM, VMEM],
        out_specs=HBM,
        out_shape=shape((NCH, 1, NB, NB), bf16),
        scratch_shapes=[pltpu.VMEM((NCH, NB, NB), bf16), pltpu.SemaphoreType.DMA((NCH,))],
        compiler_params=PARAMS,
        name="flow",
    )(received, vertex_sum, partner_row)


def solution(mesh):
    split = P(None, ("mom", "bond"), None, None)
    return jax.shard_map(
        per_device, mesh=mesh, in_specs=(split, split, P(), P(), P(), P(), P()), out_specs=split, check_vma=False
    )
```

time: 123 us -> 118 us (0.959)
  waiting for transfers between devices: 41.1 us -> 34.4 us
  Pallas kernels: 12.6 us -> 14.8 us
    all_to_all x1, waiting for transfers between devices: 41.1 us -> 34.4 us  [per_device(): lax.all_to_all(sent.reshape(Q, NCH, SUB, LANES), AXES, 0, 0, tiled=True)]
    pallas_call x3 -> x4, Pallas kernels: 12.6 us -> 14.8 us  [the longest x1 6.04 us: per_device(): pl.pallas_call(product_kernel, in_specs=[HBM, HBM, VMEM], out_specs=HBM,...]
    unnamed x20 -> x18, local copies, waits for them, and re-layouts: 5.14 us -> 4.41 us
  transfers between devices with their start and end apart: 1 -> 1, of which waited for: 1 -> 1; matrix products, arithmetic and copies ran while one was open for 0% -> 0% of each run, Pallas kernels for 0% -> 3%
where the time goes in v2:
time: 118 us
  blocking collectives  48.4 us (41%)
  waiting for transfers between devices  34.4 us (29%)
  starting transfers between devices  15.7 us (13%)
  Pallas kernels  14.8 us (13%)
  local copies, waits for them, and re-layouts  4.41 us (4%)
    all_to_all x1, blocking collectives, per_device(): received = lax.all_to_all(back, AXES, 0, 0, tiled=True).reshape(TILES)  48.4 us
    all_to_all x1, waiting for transfers between devices, per_device(): lax.all_to_all(sent.reshape(Q, NCH, SUB, LANES), AXES, 0, 0, tiled=True)  34.4 us
    all_to_all x1, starting transfers between devices, per_device(): lax.all_to_all(sent.reshape(Q, NCH, SUB, LANES), AXES, 0, 0, tiled=True)  15.7 us
    pallas_call x1, Pallas kernels, per_device(): pl.pallas_call(product_kernel, in_specs=[HBM, HBM, VMEM], out_specs=HBM,...  6.04 us
    unnamed x18, local copies, waits for them, and re-layouts  4.41 us
    pallas_call x1, Pallas kernels, per_device(): pl.pallas_call(lattice_kernel, in_specs=[SMEM] * 5 + [VMEM] * 4, out_spec...  4.06 us
    pallas_call x1, Pallas kernels, per_device(): pl.pallas_call(side_kernel, in_specs=[SMEM, HBM, HBM, VMEM, VMEM, VMEM],...  2.95 us
  transfers between devices with their start and end apart: 1, of which 1 were waited for; matrix products, arithmetic and copies ran while one was open for 0% of the time, Pallas kernels for 3%

profile of v2, /device:TPU:1, one launch (start us, length us, event | category | flops | bytes accessed | tf_op | source)
XLA Modules:
  0.0 117.8 jit_solution(10563983265208591979)
XLA Ops:
  0.0 6.0 %product.1 = bf16[32,2,4,3,8,128]{5,4,3,2,1,0:T(8,128)(2,1)} custom-call(bf16[3,1,512,512]{3,2,1,0:T(8,128)(2,1)} %vertex_hbm.3, bf16[3,1,512,512]{3,2,1,0:T(8,128)(2,1)} %loop_hbm.3, s32[1,512]{1,0:T(1,128)} %bitcast.9), custom_call_target="tpu_custom_call" | custom-call | tf_op jit(solution)/shard_map/product/pallas_call | solution.py:203
  6.0 0.0 copy-start
  6.1 0.0 copy-start.4
  6.1 0.0 copy-start.5
  6.1 15.7 %all-to-all-start = ((bf16[256,3,8,128]{3,2,1,0:T(8,128)(2,1)}), bf16[256,3,8,128]{3,2,1,0:T(8,128)(2,1)S(1)}, u32[]{:S(2)}, u32[]{:S(2)}) async-start(bf16[256,3,8,128]{3,2,1,0:T(8,128)(2,1)} %bitcast.14), calls=%async_computation | async-start | bytes 3145728 | tf_op jit(solution)/shard_map/all_to_all | solution.py:212
  21.8 0.0 copy-done
  21.8 0.0 copy-done.4
  21.8 0.0 copy-done.5
  21.8 0.0 copy-start.1
  21.8 1.4 %copy-done.1 = bf16[3,1,512,512]{3,2,1,0:T(8,128)(2,1)S(1)} copy-done((bf16[3,1,512,512]{3,2,1,0:T(8,128)(2,1)S(1)}, bf16[3,1,512,512]{3,2,1,0:T(8,128)(2,1)}, u32[]{:S(2)}) %copy-start.1) | copy-done | bytes 1572888
  23.2 0.0 copy-start.8
  23.2 0.7 copy-done.8
  23.9 0.0 copy-start.6
  23.9 2.9 %side.1 = (f32[3,512,512]{2,1,0:T(8,128)S(1)}, bf16[512,256]{1,0:T(8,128)(2,1)S(1)}, bf16[256,256]{1,0:T(8,128)(2,1)S(1)}, s32[8,128]{1,0:T(8,128)S(1)}) custom-call(s32[1]{0:T(128)} %bitcast.3.tile_col_ref, bf16[3,1,512,512]{3,2,1,0:T(8,128)(2,1)S(1)} %copy-done, bf16[3,1,512,512]{3,2,1,0:T(8,128)(2,1)S(1)} %copy-done.1, s32[1,256]{1,0:T(1,128)S(1)} %bitcast.13, ...), custom_call_target="tpu_custom_call" | custom-call | tf_op jit(solution)/shard_map/side/pallas_call | solution.py:213
  26.9 0.0 copy-start.2
  26.9 1.6 %copy-done.2 = f32[3,512,512]{2,1,0:T(8,128)} copy-done((f32[3,512,512]{2,1,0:T(8,128)}, f32[3,512,512]{2,1,0:T(8,128)S(1)}, u32[]{:S(2)}) %copy-start.2) | copy-done | bytes 3145752
  28.5 34.4 %all-to-all-done.arrived_ref = bf16[256,3,8,128]{3,2,1,0:T(8,128)(2,1)S(1)} async-done(((bf16[256,3,8,128]{3,2,1,0:T(8,128)(2,1)}), bf16[256,3,8,128]{3,2,1,0:T(8,128)(2,1)S(1)}, u32[]{:S(2)}, u32[]{:S(2)}) %all-to-all-start) | async-done | bytes 1572896 | tf_op jit(solution)/shard_map/all_to_all | solution.py:212
  62.9 0.0 copy-done.6
  62.9 0.0 copy-start.7
  62.9 0.7 copy-done.7
  63.6 4.1 %lattice.1 = bf16[256,3,8,128]{3,2,1,0:T(8,128)(2,1)S(1)} custom-call(s32[1]{0:T(128)} %bitcast.tile_row_ref, f32[3,3]{1,0:T(4,128)S(1)} %copy-done.6, f32[3,3]{1,0:T(4,128)S(1)} %copy-done.7, s32[512]{0:T(512)S(1)} %copy-done.5, s32[512]{0:T(512)S(1)} %copy-done.4, bf16[256,3,8,128]{3,2,1,0:T(8,128)(2,1)S(1)} %all-to-all-done.arrived_ref, ...), custom_call_target="tpu_custom_call" | custom-call | tf_op jit(solution)/shard_map/lattice/pallas_call | solution.py:225
  67.6 0.0 copy-start.3
  67.6 48.4 %all_to_all.10 = bf16[256,3,8,128]{3,2,1,0:T(8,128)(2,1)S(1)} all-to-all(bf16[256,3,8,128]{3,2,1,0:T(8,128)(2,1)S(1)} %lattice.1), channel_id=1, replica_groups=mesh['mom'=16,'bond'=16] {'mom','bond'}, dimensions={0} | all-to-all | bytes 3145728 | tf_op jit(solution)/shard_map/all_to_all | solution.py:234
  116.0 0.0 copy-done.3
  116.0 1.8 %flow.1 = bf16[3,1,512,512]{3,2,1,0:T(8,128)(2,1)} custom-call(bf16[32,2,4,3,8,128]{5,4,3,2,1,0:T(8,128)(2,1)S(1)} %bitcast.8, f32[3,512,512]{2,1,0:T(8,128)S(1)} %copy-done.3, s32[1,512]{1,0:T(1,128)S(1)} %bitcast.11), custom_call_target="tpu_custom_call" | custom-call | tf_op jit(solution)/shard_map/flow/pallas_call | solution.py:235
Async XLA Ops:
  6.0 15.7 %copy-start = (bf16[3,1,512,512]{3,2,1,0:T(8,128)(2,1)S(1)}, bf16[3,1,512,512]{3,2,1,0:T(8,128)(2,1)}, u32[]{:S(2)}) copy-start(bf16[3,1,512,512]{3,2,1,0:T(8,128)(2,1)} %vertex_hbm.3) | copy-start | bytes 4718596
  6.1 15.7 %copy-start.4 = (s32[512]{0:T(512)S(1)}, s32[512]{0:T(512)}, u32[]{:S(2)}) copy-start(s32[512]{0:T(512)} %partner_s.1) | copy-start | bytes 6148
  6.1 15.7 %copy-start.5 = (s32[512]{0:T(512)S(1)}, s32[512]{0:T(512)}, u32[]{:S(2)}) copy-start(s32[512]{0:T(512)} %shells_s.1) | copy-start | bytes 6148
  6.1 56.8 %all-to-all-start = ((bf16[256,3,8,128]{3,2,1,0:T(8,128)(2,1)}), bf16[256,3,8,128]{3,2,1,0:T(8,128)(2,1)S(1)}, u32[]{:S(2)}, u32[]{:S(2)}) async-start(bf16[256,3,8,128]{3,2,1,0:T(8,128)(2,1)} %bitcast.14), calls=%async_computation | async-start | bytes 3145728 | tf_op jit(solution)/shard_map/all_to_all | solution.py:212
  21.8 1.4 %copy-start.1 = (bf16[3,1,512,512]{3,2,1,0:T(8,128)(2,1)S(1)}, bf16[3,1,512,512]{3,2,1,0:T(8,128)(2,1)}, u32[]{:S(2)}) copy-start(bf16[3,1,512,512]{3,2,1,0:T(8,128)(2,1)} %loop_hbm.3) | copy-start | bytes 4718596
  23.2 0.7 copy-start.8
  23.9 39.0 %copy-start.6 = (f32[3,3]{1,0:T(4,128)S(1)}, f32[3,3]{1,0:T(4,128)}, u32[]{:S(2)}) copy-start(f32[3,3]{1,0:T(4,128)} %own_mix_ref.1) | copy-start | bytes 112
  26.9 1.6 %copy-start.2 = (f32[3,512,512]{2,1,0:T(8,128)}, f32[3,512,512]{2,1,0:T(8,128)S(1)}, u32[]{:S(2)}) copy-start(f32[3,512,512]{2,1,0:T(8,128)S(1)} %get-tuple-element.12.sum_ref) | copy-start | bytes 9437188
  62.9 0.7 copy-start.7
  67.6 48.4 %copy-start.3 = (f32[3,512,512]{2,1,0:T(8,128)S(1)}, f32[3,512,512]{2,1,0:T(8,128)}, u32[]{:S(2)}) copy-start(f32[3,512,512]{2,1,0:T(8,128)} %copy-done.2) | copy-start | bytes 9437188

commit v3 on v2

--- a/solution.py
+++ b/solution.py
@@ -18,6 +18,9 @@
 PAIR = SUB // 2
 TILES = (HALF // SUB, 2, TILE_COLS, NCH, SUB, LANES)
 AXES = ("mom", "bond")
+LIMITS = 0
+GAINS = LIMITS + SUB
+ROWS = GAINS + SUB
 
 CAS = [math.cos(2 * math.pi * n / G) + math.sin(2 * math.pi * n / G) for n in range(8)]
 CAS[6] = 0.0
@@ -106,26 +109,44 @@
     return jnp.where(phase & 8 != 0, -value, value)
 
 
+def gain_lane(crossed, to, source):
+    return (crossed * NCH + to) * NCH + source
+
+
 def side_kernel(
-    tile_col_ref, vertex_hbm, loop_hbm, grid_ref, shells_ref, partner_ref, sum_ref, tables_ref, back_ref, shell_rows_ref,
-    vertex_buf, loop_buf, sems,
+    place_ref, own_mix_ref, cross_mix_ref, shells_s, partner_s, vertex_hbm, loop_hbm, grid_ref, shells_ref, partner_ref,
+    sum_ref, squares_ref, rows_ref, vertex_buf, loop_buf, sems,
 ):
     copies = fetch([(vertex_hbm, vertex_buf), (loop_hbm, loop_buf)], sems)
+    tile_row = place_ref[0] // TILE_COLS
+    tile_col = place_ref[0] % TILE_COLS
     point = grid_ref[...]
     disp = iota((Q, Q), 0)
     phase = (disp // G) * (point // G) + (disp % G) * (point % G)
     plus = cas_values(phase & 15)
-    tables_ref[:Q] = plus.astype(jnp.bfloat16)
-    tables_ref[Q:] = cas_values((-phase) & 15).astype(jnp.bfloat16)
-    back_ref[...] = plus.T.astype(jnp.bfloat16)
-    tile_col = tile_col_ref[0]
+    squares_ref[0] = plus.astype(jnp.bfloat16)
+    squares_ref[1] = cas_values((-phase) & 15).astype(jnp.bfloat16)
+    squares_ref[2] = plus.T.astype(jnp.bfloat16)
     pick = to_bf16(iota((NB, LANES), 0) == partner_ref[pl.ds(tile_col, 1), :])
     crossed_row = jnp.zeros((SUB, LANES), jnp.float32)
     for j in range(TILE_COLS):
         part = to_bf16(jnp.broadcast_to(shells_ref[pl.ds(j, 1), :], (SUB, LANES)))
         crossed_row += dot(part, pick[j * LANES : (j + 1) * LANES])
-    own_row = jnp.broadcast_to(shells_ref[pl.ds(tile_col, 1), :], (SUB, LANES))
-    shell_rows_ref[...] = jnp.where(iota((SUB, LANES), 0) < PAIR, own_row, crossed_row.astype(jnp.int32))
+    crossed_row = crossed_row[:1]
+    own_row = shells_ref[pl.ds(tile_col, 1), :].astype(jnp.float32)
+    for s in range(PAIR):
+        bond = tile_row * PAIR + s
+        rows_ref[LIMITS + s : LIMITS + s + 1, :] = own_row + shells_s[bond].astype(jnp.float32)
+        rows_ref[LIMITS + PAIR + s : LIMITS + PAIR + s + 1, :] = (
+            crossed_row + shells_s[partner_s[bond]].astype(jnp.float32)
+        )
+    lane = iota((SUB, LANES), 1)
+    gains = jnp.zeros((SUB, LANES), jnp.float32)
+    for d in range(NCH):
+        for c in range(NCH):
+            gains = jnp.where(lane == gain_lane(0, d, c), own_mix_ref[d, c] * (1.0 / Q), gains)
+            gains = jnp.where(lane == gain_lane(1, d, c), cross_mix_ref[d, c] * (1.0 / Q), gains)
+    rows_ref[GAINS:] = gains
     for c in range(NCH):
         for copy in copies[c]:
             copy.wait()
@@ -133,38 +154,37 @@
         sum_ref[c] = vertex.astype(jnp.float32) + product_of(vertex, loop_buf[c])
 
 
-def lattice_kernel(
-    tile_row_ref, own_mix_ref, cross_mix_ref, shells_s, partner_s, arrived_ref, tables_ref, plus_back_ref,
-    shell_rows_ref, back_ref, in_ref, out_ref,
-):
-    tile_row = tile_row_ref[0]
+def lattice_kernel(arrived_ref, squares_ref, rows_ref, back_ref, in_ref, out_ref):
     lattice_point = iota((Q, LANES), 0)
     centre_x = (lattice_point // G + G // 2) % G - G // 2
     centre_y = (lattice_point % G + G // 2) % G - G // 2
-    cycle = jnp.maximum(jnp.abs(centre_x), jnp.abs(centre_y))
+    cycle = jnp.maximum(jnp.abs(centre_x), jnp.abs(centre_y)).astype(jnp.float32)
+    tables = squares_ref[:2].reshape(2 * Q, Q)
+    gains = rows_ref[GAINS : GAINS + 1, :]
     for c in range(NCH):
         in_ref[c] = arrived_ref[:, c].astype(jnp.float32).reshape(Q * SUB, LANES)
     for s in range(PAIR):
-        bond = tile_row * PAIR + s
-        own_keep = cycle <= shell_rows_ref[0:1, :] + shells_s[bond]
-        cross_keep = cycle <= shell_rows_ref[PAIR : PAIR + 1, :] + shells_s[partner_s[bond]]
+        own_keep = cycle <= rows_ref[LIMITS + s : LIMITS + s + 1, :]
+        cross_keep = cycle <= rows_ref[LIMITS + PAIR + s : LIMITS + PAIR + s + 1, :]
         lattice = []
         for c in range(NCH):
             own = in_ref[c, pl.ds(s, Q, stride=SUB), :].astype(jnp.bfloat16)
             crossed = in_ref[c, pl.ds(s + PAIR, Q, stride=SUB), :].astype(jnp.bfloat16)
-            lattice.append(dot(tables_ref[...], jnp.concatenate([own, crossed], axis=1)))
+            lattice.append(dot(tables, jnp.concatenate([own, crossed], axis=1)))
         for d in range(NCH):
             own_sum = jnp.zeros((Q, LANES), jnp.float32)
             cross_sum = jnp.zeros((Q, LANES), jnp.float32)
             for c in range(NCH):
-                own_gain = own_mix_ref[d, c] * (1.0 / Q)
-                cross_gain = cross_mix_ref[d, c] * (1.0 / Q)
+                at = gain_lane(0, d, c)
+                own_gain = gains[:, at : at + 1]
+                at = gain_lane(1, d, c)
+                cross_gain = gains[:, at : at + 1]
                 own_sum += own_gain * lattice[c][:Q, :LANES] + cross_gain * lattice[c][Q:, LANES:]
                 cross_sum += own_gain * lattice[c][:Q, LANES:] + cross_gain * lattice[c][Q:, :LANES]
             projected = jnp.concatenate(
                 [jnp.where(own_keep, own_sum, 0.0), jnp.where(cross_keep, cross_sum, 0.0)], axis=1
             ).astype(jnp.bfloat16)
-            returned = dot(plus_back_ref[...], projected)
+            returned = dot(squares_ref[2], projected)
             out_ref[d, pl.ds(s, Q, stride=SUB), :] = returned[:, :LANES]
             out_ref[d, pl.ds(s + PAIR, Q, stride=SUB), :] = returned[:, LANES:]
     for d in range(NCH):
@@ -199,7 +219,7 @@
         pltpu.SemaphoreType.DMA((2, NCH)),
     ]
     partner_row = partner.reshape(1, NB)
-    place = lax.axis_index(AXES).astype(i32)
+    place = lax.axis_index(AXES).astype(i32).reshape(1)
     sent = pl.pallas_call(
         product_kernel,
         in_specs=[HBM, HBM, VMEM],
@@ -210,27 +230,27 @@
         name="product",
     )(vertex, loop_matrix, partner_row)
     arrived = lax.all_to_all(sent.reshape(Q, NCH, SUB, LANES), AXES, 0, 0, tiled=True)
-    vertex_sum, tables, plus_back, shell_rows = pl.pallas_call(
+    vertex_sum, squares, rows = pl.pallas_call(
         side_kernel,
-        in_specs=[SMEM, HBM, HBM, VMEM, VMEM, VMEM],
-        out_specs=[VMEM] * 4,
-        out_shape=[shape((NCH, NB, NB), f32), shape((2 * Q, Q), bf16), shape((Q, Q), bf16), shape((SUB, LANES), i32)],
+        in_specs=[SMEM] * 5 + [HBM, HBM] + [VMEM] * 3,
+        out_specs=[VMEM] * 3,
+        out_shape=[shape((NCH, NB, NB), f32), shape((3, Q, Q), bf16), shape((ROWS, LANES), f32)],
         scratch_shapes=fetched,
         compiler_params=PARAMS,
         name="side",
     )(
-        (place % TILE_COLS).reshape(1), vertex, loop_matrix, grid_index.reshape(1, Q),
+        place, own_mix, cross_mix, shells, partner, vertex, loop_matrix, grid_index.reshape(1, Q),
         shells.reshape(TILE_COLS, LANES), partner.reshape(TILE_COLS, LANES),
     )
     back = pl.pallas_call(
         lattice_kernel,
-        in_specs=[SMEM] * 5 + [VMEM] * 4,
+        in_specs=[VMEM] * 3,
         out_specs=VMEM,
         out_shape=shape((Q, NCH, SUB, LANES), bf16),
         scratch_shapes=[pltpu.VMEM((NCH, Q * SUB, LANES), f32), pltpu.VMEM((NCH, Q * SUB, LANES), f32)],
         compiler_params=PARAMS,
         name="lattice",
-    )((place // TILE_COLS).reshape(1), own_mix, cross_mix, shells, partner, arrived, tables, plus_back, shell_rows)
+    )(arrived, squares, rows)
     received = lax.all_to_all(back, AXES, 0, 0, tiled=True).reshape(TILES)
     return pl.pallas_call(
         flow_kernel,

time: 118 us -> 117 us (level)
  waiting for transfers between devices: 34.4 us -> 32.4 us
    all_to_all x1, waiting for transfers between devices: 34.4 us -> 32.4 us  [per_device(): lax.all_to_all(sent.reshape(Q, NCH, SUB, LANES), AXES, 0, 0, tiled=True)]
where the time goes in v3:
time: 117 us
  blocking collectives  48.4 us (41%)
  waiting for transfers between devices  32.4 us (28%)
  starting transfers between devices  15.7 us (13%)
  Pallas kernels  15 us (13%)
  local copies, waits for them, and re-layouts  5.09 us (4%)
    all_to_all x1, blocking collectives, per_device(): received = lax.all_to_all(back, AXES, 0, 0, tiled=True).reshape(TILES)  48.4 us
    all_to_all x1, waiting for transfers between devices, per_device(): lax.all_to_all(sent.reshape(Q, NCH, SUB, LANES), AXES, 0, 0, tiled=True)  32.4 us
    all_to_all x1, starting transfers between devices, per_device(): lax.all_to_all(sent.reshape(Q, NCH, SUB, LANES), AXES, 0, 0, tiled=True)  15.7 us
    pallas_call x1, Pallas kernels, per_device(): pl.pallas_call(product_kernel, in_specs=[HBM, HBM, VMEM], out_specs=HBM,...  6.04 us
    unnamed x18, local copies, waits for them, and re-layouts  5.09 us
    pallas_call x1, Pallas kernels, per_device(): pl.pallas_call(side_kernel, in_specs=[SMEM] * 5 + [HBM, HBM] + [VMEM] * 3...  3.62 us
    pallas_call x1, Pallas kernels, per_device(): pl.pallas_call(lattice_kernel, in_specs=[VMEM] * 3, out_specs=VMEM, out_s...  3.53 us
  transfers between devices with their start and end apart: 1, of which 1 were waited for; matrix products, arithmetic and copies ran while one was open for 0% of the time, Pallas kernels for 3%

profile of v3, /device:TPU:1, one launch (start us, length us, event | category | flops | bytes accessed | tf_op | source)
XLA Modules:
  0.0 116.6 jit_solution(16908879544136058280)
XLA Ops:
  0.0 6.0 %product.1 = bf16[32,2,4,3,8,128]{5,4,3,2,1,0:T(8,128)(2,1)} custom-call(bf16[3,1,512,512]{3,2,1,0:T(8,128)(2,1)} %vertex_hbm.3, bf16[3,1,512,512]{3,2,1,0:T(8,128)(2,1)} %loop_hbm.3, s32[1,512]{1,0:T(1,128)} %bitcast.8), custom_call_target="tpu_custom_call" | custom-call | tf_op jit(solution)/shard_map/product/pallas_call | solution.py:223
  6.0 0.0 copy-start
  6.1 0.0 copy-start.4
  6.1 0.0 copy-start.5
  6.1 15.7 %all-to-all-start = ((bf16[256,3,8,128]{3,2,1,0:T(8,128)(2,1)}), bf16[256,3,8,128]{3,2,1,0:T(8,128)(2,1)S(1)}, u32[]{:S(2)}, u32[]{:S(2)}) async-start(bf16[256,3,8,128]{3,2,1,0:T(8,128)(2,1)} %bitcast.13), calls=%async_computation | async-start | bytes 3145728 | tf_op jit(solution)/shard_map/all_to_all | solution.py:232
  21.8 0.0 copy-done
  21.8 0.0 copy-done.4
  21.8 0.0 copy-done.5
  21.8 0.0 copy-start.1
  21.8 1.4 %copy-done.1 = bf16[3,1,512,512]{3,2,1,0:T(8,128)(2,1)S(1)} copy-done((bf16[3,1,512,512]{3,2,1,0:T(8,128)(2,1)S(1)}, bf16[3,1,512,512]{3,2,1,0:T(8,128)(2,1)}, u32[]{:S(2)}) %copy-start.1) | copy-done | bytes 1572888
  23.2 0.0 copy-start.6
  23.2 0.7 copy-done.6
  23.9 0.0 copy-start.7
  23.9 0.7 copy-done.7
  24.6 0.0 copy-start.8
  24.6 0.7 copy-done.8
  25.3 3.6 %side.1 = (f32[3,512,512]{2,1,0:T(8,128)S(1)}, bf16[3,256,256]{2,1,0:T(8,128)(2,1)S(1)}, f32[16,128]{1,0:T(8,128)S(1)}) custom-call(s32[1]{0:T(128)} %bitcast.2.place_ref, f32[3,3]{1,0:T(4,128)S(1)} %copy-done.6, f32[3,3]{1,0:T(4,128)S(1)} %copy-done.7, s32[512]{0:T(512)S(1)} %copy-done.5, s32[512]{0:T(512)S(1)} %copy-done.4, ...), custom_call_target="tpu_custom_call" | custom-call | tf_op jit(solution)/shard_map/side/pallas_call | solution.py:233
  28.9 0.0 copy-start.2
  28.9 1.6 %copy-done.2 = f32[3,512,512]{2,1,0:T(8,128)} copy-done((f32[3,512,512]{2,1,0:T(8,128)}, f32[3,512,512]{2,1,0:T(8,128)S(1)}, u32[]{:S(2)}) %copy-start.2) | copy-done | bytes 3145752
  30.5 32.4 %all-to-all-done.arrived_ref = bf16[256,3,8,128]{3,2,1,0:T(8,128)(2,1)S(1)} async-done(((bf16[256,3,8,128]{3,2,1,0:T(8,128)(2,1)}), bf16[256,3,8,128]{3,2,1,0:T(8,128)(2,1)S(1)}, u32[]{:S(2)}, u32[]{:S(2)}) %all-to-all-start) | async-done | bytes 1572896 | tf_op jit(solution)/shard_map/all_to_all | solution.py:232
  62.9 3.5 %lattice.1 = bf16[256,3,8,128]{3,2,1,0:T(8,128)(2,1)S(1)} custom-call(bf16[256,3,8,128]{3,2,1,0:T(8,128)(2,1)S(1)} %all-to-all-done.arrived_ref, bf16[3,256,256]{2,1,0:T(8,128)(2,1)S(1)} %get-tuple-element.8.squares_ref, f32[16,128]{1,0:T(8,128)S(1)} %get-tuple-element.9.rows_ref), custom_call_target="tpu_custom_call" | custom-call | tf_op jit(solution)/shard_map/lattice/pallas_call | solution.py:245
  66.4 0.0 copy-start.3
  66.4 48.4 %all_to_all.10 = bf16[256,3,8,128]{3,2,1,0:T(8,128)(2,1)S(1)} all-to-all(bf16[256,3,8,128]{3,2,1,0:T(8,128)(2,1)S(1)} %lattice.1), channel_id=1, replica_groups=mesh['mom'=16,'bond'=16] {'mom','bond'}, dimensions={0} | all-to-all | bytes 3145728 | tf_op jit(solution)/shard_map/all_to_all | solution.py:254
  114.8 0.0 copy-done.3
  114.8 1.8 %flow.1 = bf16[3,1,512,512]{3,2,1,0:T(8,128)(2,1)} custom-call(bf16[32,2,4,3,8,128]{5,4,3,2,1,0:T(8,128)(2,1)S(1)} %bitcast.7, f32[3,512,512]{2,1,0:T(8,128)S(1)} %copy-done.3, s32[1,512]{1,0:T(1,128)S(1)} %bitcast.10), custom_call_target="tpu_custom_call" | custom-call | tf_op jit(solution)/shard_map/flow/pallas_call | solution.py:255
Async XLA Ops:
  6.0 15.7 %copy-start = (bf16[3,1,512,512]{3,2,1,0:T(8,128)(2,1)S(1)}, bf16[3,1,512,512]{3,2,1,0:T(8,128)(2,1)}, u32[]{:S(2)}) copy-start(bf16[3,1,512,512]{3,2,1,0:T(8,128)(2,1)} %vertex_hbm.3) | copy-start | bytes 4718596
  6.1 15.7 %copy-start.4 = (s32[512]{0:T(512)S(1)}, s32[512]{0:T(512)}, u32[]{:S(2)}) copy-start(s32[512]{0:T(512)} %partner_s.1) | copy-start | bytes 6148
  6.1 15.7 %copy-start.5 = (s32[512]{0:T(512)S(1)}, s32[512]{0:T(512)}, u32[]{:S(2)}) copy-start(s32[512]{0:T(512)} %shells_s.1) | copy-start | bytes 6148
  6.1 56.8 %all-to-all-start = ((bf16[256,3,8,128]{3,2,1,0:T(8,128)(2,1)}), bf16[256,3,8,128]{3,2,1,0:T(8,128)(2,1)S(1)}, u32[]{:S(2)}, u32[]{:S(2)}) async-start(bf16[256,3,8,128]{3,2,1,0:T(8,128)(2,1)} %bitcast.13), calls=%async_computation | async-start | bytes 3145728 | tf_op jit(solution)/shard_map/all_to_all | solution.py:232
  21.8 1.4 %copy-start.1 = (bf16[3,1,512,512]{3,2,1,0:T(8,128)(2,1)S(1)}, bf16[3,1,512,512]{3,2,1,0:T(8,128)(2,1)}, u32[]{:S(2)}) copy-start(bf16[3,1,512,512]{3,2,1,0:T(8,128)(2,1)} %loop_hbm.3) | copy-start | bytes 4718596
  23.2 0.7 copy-start.6
  23.9 0.7 copy-start.7
  24.6 0.7 copy-start.8
  28.9 1.6 %copy-start.2 = (f32[3,512,512]{2,1,0:T(8,128)}, f32[3,512,512]{2,1,0:T(8,128)S(1)}, u32[]{:S(2)}) copy-start(f32[3,512,512]{2,1,0:T(8,128)S(1)} %get-tuple-element.10.sum_ref) | copy-start | bytes 9437188
  66.4 48.4 %copy-start.3 = (f32[3,512,512]{2,1,0:T(8,128)S(1)}, f32[3,512,512]{2,1,0:T(8,128)}, u32[]{:S(2)}) copy-start(f32[3,512,512]{2,1,0:T(8,128)} %copy-done.2) | copy-start | bytes 9437188

commit v4 on v3

--- a/solution.py
+++ b/solution.py
@@ -82,23 +82,18 @@
     return copies
 
 
-def product_kernel(vertex_hbm, loop_hbm, partner_ref, sent_hbm, vertex_buf, loop_buf, sems, sent_ref, sent_sems):
-    copies = fetch([(vertex_hbm, vertex_buf), (loop_hbm, loop_buf)], sems)
-    upper_of, lower_of = partner_blocks(partner_ref)
-    sends = []
-    for c in range(NCH):
-        for copy in copies[c]:
-            copy.wait()
-        product = product_of(vertex_buf[c], loop_buf[c])
-        swapped = swap_columns(product[HALF:], upper_of, lower_of).astype(jnp.bfloat16)
-        crossed = dot(upper_of, swapped)
-        for half, rows in enumerate(interleave(by_groups(product[:HALF]), by_groups(crossed))):
-            for j in range(TILE_COLS):
-                sent_ref[:, half, j, c] = rows[:, :, j * LANES : (j + 1) * LANES].astype(jnp.bfloat16)
-        sends.append(pltpu.make_async_copy(sent_ref.at[:, :, :, c], sent_hbm.at[:, :, :, c], sent_sems.at[c]))
-        sends[c].start()
-    for copy in sends:
-        copy.wait()
+def product_kernel(vertex_ref, loop_ref, partner_ref, sent_ref, upper_ref, lower_ref):
+    @pl.when(pl.program_id(0) == 0)
+    def _():
+        upper_ref[...], lower_ref[...] = partner_blocks(partner_ref)
+
+    upper_of, lower_of = upper_ref[...], lower_ref[...]
+    product = product_of(vertex_ref[0, 0], loop_ref[0, 0])
+    swapped = swap_columns(product[HALF:], upper_of, lower_of).astype(jnp.bfloat16)
+    crossed = dot(upper_of, swapped)
+    for half, rows in enumerate(interleave(by_groups(product[:HALF]), by_groups(crossed))):
+        for j in range(TILE_COLS):
+            sent_ref[:, half, j, 0] = rows[:, :, j * LANES : (j + 1) * LANES].astype(jnp.bfloat16)
 
 
 def cas_values(phase):
@@ -162,7 +157,7 @@
     tables = squares_ref[:2].reshape(2 * Q, Q)
     gains = rows_ref[GAINS : GAINS + 1, :]
     for c in range(NCH):
-        in_ref[c] = arrived_ref[:, c].astype(jnp.float32).reshape(Q * SUB, LANES)
+        in_ref[c, : Q * SUB] = arrived_ref[:, c].astype(jnp.float32).reshape(Q * SUB, LANES)
     for s in range(PAIR):
         own_keep = cycle <= rows_ref[LIMITS + s : LIMITS + s + 1, :]
         cross_keep = cycle <= rows_ref[LIMITS + PAIR + s : LIMITS + PAIR + s + 1, :]
@@ -188,7 +183,7 @@
             out_ref[d, pl.ds(s, Q, stride=SUB), :] = returned[:, :LANES]
             out_ref[d, pl.ds(s + PAIR, Q, stride=SUB), :] = returned[:, LANES:]
     for d in range(NCH):
-        back_ref[:, d] = out_ref[d].reshape(Q, SUB, LANES).astype(jnp.bfloat16)
+        back_ref[:, d] = out_ref[d, : Q * SUB].reshape(Q, SUB, LANES).astype(jnp.bfloat16)
 
 
 def flow_kernel(received_ref, sum_ref, partner_ref, flowed_hbm, flowed_buf, sems):
@@ -218,14 +213,17 @@
         pltpu.VMEM((NCH, NB, NB), bf16),
         pltpu.SemaphoreType.DMA((2, NCH)),
     ]
+    strided = pltpu.VMEM((NCH, Q * SUB + SUB, LANES), f32)
     partner_row = partner.reshape(1, NB)
     place = lax.axis_index(AXES).astype(i32).reshape(1)
+    matrix_spec = pl.BlockSpec((1, 1, NB, NB), lambda c: (c, 0, 0, 0))
     sent = pl.pallas_call(
         product_kernel,
-        in_specs=[HBM, HBM, VMEM],
-        out_specs=HBM,
+        grid=(NCH,),
+        in_specs=[matrix_spec, matrix_spec, pl.BlockSpec((1, NB), lambda c: (0, 0))],
+        out_specs=pl.BlockSpec((*TILES[:3], 1, SUB, LANES), lambda c: (0, 0, 0, c, 0, 0)),
         out_shape=shape(TILES, bf16),
-        scratch_shapes=[*fetched, pltpu.VMEM(TILES, bf16), pltpu.SemaphoreType.DMA((NCH,))],
+        scratch_shapes=[pltpu.VMEM((HALF, HALF), bf16), pltpu.VMEM((HALF, HALF), bf16)],
         compiler_params=FULL,
         name="product",
     )(vertex, loop_matrix, partner_row)
@@ -247,7 +245,7 @@
         in_specs=[VMEM] * 3,
         out_specs=VMEM,
         out_shape=shape((Q, NCH, SUB, LANES), bf16),
-        scratch_shapes=[pltpu.VMEM((NCH, Q * SUB, LANES), f32), pltpu.VMEM((NCH, Q * SUB, LANES), f32)],
+        scratch_shapes=[strided, strided],
         compiler_params=PARAMS,
         name="lattice",
     )(arrived, squares, rows)

time: 117 us -> 116 us (level)
  no operation moved by 1% of the time
where the time goes in v4:
time: 116 us
  blocking collectives  48.4 us (42%)
  waiting for transfers between devices  32.4 us (28%)
  starting transfers between devices  15.7 us (14%)
  Pallas kernels  14.6 us (13%)
  local copies, waits for them, and re-layouts  5.08 us (4%)
    all_to_all x1, blocking collectives, per_device(): received = lax.all_to_all(back, AXES, 0, 0, tiled=True).reshape(TILES)  48.4 us
    all_to_all x1, waiting for transfers between devices, per_device(): lax.all_to_all(sent.reshape(Q, NCH, SUB, LANES), AXES, 0, 0, tiled=True)  32.4 us
    all_to_all x1, starting transfers between devices, per_device(): lax.all_to_all(sent.reshape(Q, NCH, SUB, LANES), AXES, 0, 0, tiled=True)  15.7 us
    pallas_call x1, Pallas kernels, per_device(): pl.pallas_call(product_kernel, grid=(NCH,), in_specs=[matrix_spec, matrix...  5.62 us
    unnamed x18, local copies, waits for them, and re-layouts  5.08 us
    pallas_call x1, Pallas kernels, per_device(): pl.pallas_call(side_kernel, in_specs=[SMEM] * 5 + [HBM, HBM] + [VMEM] * 3...  3.62 us
    pallas_call x1, Pallas kernels, per_device(): pl.pallas_call(lattice_kernel, in_specs=[VMEM] * 3, out_specs=VMEM, out_s...  3.53 us
  transfers between devices with their start and end apart: 1, of which 1 were waited for; matrix products, arithmetic and copies ran while one was open for 0% of the time, Pallas kernels for 3%

profile of v4, /device:TPU:1, one launch (start us, length us, event | category | flops | bytes accessed | tf_op | source)
XLA Modules:
  0.0 116.1 jit_solution(6055192031807992431)
XLA Ops:
  0.0 5.6 %product.1 = bf16[32,2,4,3,8,128]{5,4,3,2,1,0:T(8,128)(2,1)} custom-call(bf16[3,1,512,512]{3,2,1,0:T(8,128)(2,1)} %vertex_hbm.1, bf16[3,1,512,512]{3,2,1,0:T(8,128)(2,1)} %loop_hbm.1, s32[1,512]{1,0:T(1,128)} %bitcast.8), custom_call_target="tpu_custom_call" | custom-call | tf_op jit(solution)/shard_map/product/pallas_call | solution.py:220
  5.6 0.0 copy-start
  5.6 0.0 copy-start.4
  5.6 0.0 copy-start.5
  5.6 15.7 %all-to-all-start = ((bf16[256,3,8,128]{3,2,1,0:T(8,128)(2,1)}), bf16[256,3,8,128]{3,2,1,0:T(8,128)(2,1)S(1)}, u32[]{:S(2)}, u32[]{:S(2)}) async-start(bf16[256,3,8,128]{3,2,1,0:T(8,128)(2,1)} %bitcast.13), calls=%async_computation | async-start | bytes 3145728 | tf_op jit(solution)/shard_map/all_to_all | solution.py:230
  21.3 0.0 copy-done
  21.3 0.0 copy-done.4
  21.3 0.0 copy-done.5
  21.3 0.0 copy-start.1
  21.4 1.4 %copy-done.1 = bf16[3,1,512,512]{3,2,1,0:T(8,128)(2,1)S(1)} copy-done((bf16[3,1,512,512]{3,2,1,0:T(8,128)(2,1)S(1)}, bf16[3,1,512,512]{3,2,1,0:T(8,128)(2,1)}, u32[]{:S(2)}) %copy-start.1) | copy-done | bytes 1572888
  22.8 0.0 copy-start.6
  22.8 0.7 copy-done.6
  23.4 0.0 copy-start.7
  23.4 0.7 copy-done.7
  24.1 0.0 copy-start.8
  24.1 0.7 copy-done.8
  24.8 3.6 %side.1 = (f32[3,512,512]{2,1,0:T(8,128)S(1)}, bf16[3,256,256]{2,1,0:T(8,128)(2,1)S(1)}, f32[16,128]{1,0:T(8,128)S(1)}) custom-call(s32[1]{0:T(128)} %bitcast.2.place_ref, f32[3,3]{1,0:T(4,128)S(1)} %copy-done.6, f32[3,3]{1,0:T(4,128)S(1)} %copy-done.7, s32[512]{0:T(512)S(1)} %copy-done.5, s32[512]{0:T(512)S(1)} %copy-done.4, ...), custom_call_target="tpu_custom_call" | custom-call | tf_op jit(solution)/shard_map/side/pallas_call | solution.py:231
  28.4 0.0 copy-start.2
  28.4 1.6 %copy-done.2 = f32[3,512,512]{2,1,0:T(8,128)} copy-done((f32[3,512,512]{2,1,0:T(8,128)}, f32[3,512,512]{2,1,0:T(8,128)S(1)}, u32[]{:S(2)}) %copy-start.2) | copy-done | bytes 3145752
  30.1 32.4 %all-to-all-done.arrived_ref = bf16[256,3,8,128]{3,2,1,0:T(8,128)(2,1)S(1)} async-done(((bf16[256,3,8,128]{3,2,1,0:T(8,128)(2,1)}), bf16[256,3,8,128]{3,2,1,0:T(8,128)(2,1)S(1)}, u32[]{:S(2)}, u32[]{:S(2)}) %all-to-all-start) | async-done | bytes 1572896 | tf_op jit(solution)/shard_map/all_to_all | solution.py:230
  62.4 3.5 %lattice.1 = bf16[256,3,8,128]{3,2,1,0:T(8,128)(2,1)S(1)} custom-call(bf16[256,3,8,128]{3,2,1,0:T(8,128)(2,1)S(1)} %all-to-all-done.arrived_ref, bf16[3,256,256]{2,1,0:T(8,128)(2,1)S(1)} %get-tuple-element.8.squares_ref, f32[16,128]{1,0:T(8,128)S(1)} %get-tuple-element.9.rows_ref), custom_call_target="tpu_custom_call" | custom-call | tf_op jit(solution)/shard_map/lattice/pallas_call | solution.py:243
  66.0 0.0 copy-start.3
  66.0 48.4 %all_to_all.10 = bf16[256,3,8,128]{3,2,1,0:T(8,128)(2,1)S(1)} all-to-all(bf16[256,3,8,128]{3,2,1,0:T(8,128)(2,1)S(1)} %lattice.1), channel_id=1, replica_groups=mesh['mom'=16,'bond'=16] {'mom','bond'}, dimensions={0} | all-to-all | bytes 3145728 | tf_op jit(solution)/shard_map/all_to_all | solution.py:252
  114.3 0.0 copy-done.3
  114.3 1.8 %flow.1 = bf16[3,1,512,512]{3,2,1,0:T(8,128)(2,1)} custom-call(bf16[32,2,4,3,8,128]{5,4,3,2,1,0:T(8,128)(2,1)S(1)} %bitcast.7, f32[3,512,512]{2,1,0:T(8,128)S(1)} %copy-done.3, s32[1,512]{1,0:T(1,128)S(1)} %bitcast.10), custom_call_target="tpu_custom_call" | custom-call | tf_op jit(solution)/shard_map/flow/pallas_call | solution.py:253
Async XLA Ops:
  5.6 15.7 %copy-start = (bf16[3,1,512,512]{3,2,1,0:T(8,128)(2,1)S(1)}, bf16[3,1,512,512]{3,2,1,0:T(8,128)(2,1)}, u32[]{:S(2)}) copy-start(bf16[3,1,512,512]{3,2,1,0:T(8,128)(2,1)} %vertex_hbm.1) | copy-start | bytes 4718596
  5.6 15.7 %copy-start.4 = (s32[512]{0:T(512)S(1)}, s32[512]{0:T(512)}, u32[]{:S(2)}) copy-start(s32[512]{0:T(512)} %partner_s.1) | copy-start | bytes 6148
  5.6 15.7 %copy-start.5 = (s32[512]{0:T(512)S(1)}, s32[512]{0:T(512)}, u32[]{:S(2)}) copy-start(s32[512]{0:T(512)} %shells_s.1) | copy-start | bytes 6148
  5.6 56.8 %all-to-all-start = ((bf16[256,3,8,128]{3,2,1,0:T(8,128)(2,1)}), bf16[256,3,8,128]{3,2,1,0:T(8,128)(2,1)S(1)}, u32[]{:S(2)}, u32[]{:S(2)}) async-start(bf16[256,3,8,128]{3,2,1,0:T(8,128)(2,1)} %bitcast.13), calls=%async_computation | async-start | bytes 3145728 | tf_op jit(solution)/shard_map/all_to_all | solution.py:230
  21.3 1.4 %copy-start.1 = (bf16[3,1,512,512]{3,2,1,0:T(8,128)(2,1)S(1)}, bf16[3,1,512,512]{3,2,1,0:T(8,128)(2,1)}, u32[]{:S(2)}) copy-start(bf16[3,1,512,512]{3,2,1,0:T(8,128)(2,1)} %loop_hbm.1) | copy-start | bytes 4718596
  22.8 0.7 copy-start.6
  23.4 0.7 copy-start.7
  24.1 0.7 copy-start.8
  28.4 1.6 %copy-start.2 = (f32[3,512,512]{2,1,0:T(8,128)}, f32[3,512,512]{2,1,0:T(8,128)S(1)}, u32[]{:S(2)}) copy-start(f32[3,512,512]{2,1,0:T(8,128)S(1)} %get-tuple-element.10.sum_ref) | copy-start | bytes 9437188
  66.0 48.4 %copy-start.3 = (f32[3,512,512]{2,1,0:T(8,128)S(1)}, f32[3,512,512]{2,1,0:T(8,128)}, u32[]{:S(2)}) copy-start(f32[3,512,512]{2,1,0:T(8,128)} %copy-done.2) | copy-start | bytes 9437188

commit v5 on v4

--- a/solution.py
+++ b/solution.py
@@ -110,9 +110,12 @@
 
 def side_kernel(
     place_ref, own_mix_ref, cross_mix_ref, shells_s, partner_s, vertex_hbm, loop_hbm, grid_ref, shells_ref, partner_ref,
-    sum_ref, squares_ref, rows_ref, vertex_buf, loop_buf, sems,
+    partner_row_ref, sum_ref, squares_ref, rows_ref, blocks_hbm, vertex_buf, loop_buf, sems, blocks_buf, blocks_sem,
 ):
     copies = fetch([(vertex_hbm, vertex_buf), (loop_hbm, loop_buf)], sems)
+    blocks_buf[0], blocks_buf[1] = partner_blocks(partner_row_ref)
+    blocks_copy = pltpu.make_async_copy(blocks_buf, blocks_hbm, blocks_sem)
+    blocks_copy.start()
     tile_row = place_ref[0] // TILE_COLS
     tile_col = place_ref[0] % TILE_COLS
     point = grid_ref[...]
@@ -147,6 +150,7 @@
             copy.wait()
         vertex = vertex_buf[c]
         sum_ref[c] = vertex.astype(jnp.float32) + product_of(vertex, loop_buf[c])
+    blocks_copy.wait()
 
 
 def lattice_kernel(arrived_ref, squares_ref, rows_ref, back_ref, in_ref, out_ref):
@@ -186,8 +190,8 @@
         back_ref[:, d] = out_ref[d, : Q * SUB].reshape(Q, SUB, LANES).astype(jnp.bfloat16)
 
 
-def flow_kernel(received_ref, sum_ref, partner_ref, flowed_hbm, flowed_buf, sems):
-    upper_of, lower_of = partner_blocks(partner_ref)
+def flow_kernel(received_ref, sum_ref, blocks_ref, flowed_hbm, flowed_buf, sems):
+    upper_of, lower_of = blocks_ref[0], blocks_ref[1]
     copies = []
     for c in range(NCH):
         halves = [
@@ -228,17 +232,17 @@
         name="product",
     )(vertex, loop_matrix, partner_row)
     arrived = lax.all_to_all(sent.reshape(Q, NCH, SUB, LANES), AXES, 0, 0, tiled=True)
-    vertex_sum, squares, rows = pl.pallas_call(
+    vertex_sum, squares, rows, blocks = pl.pallas_call(
         side_kernel,
-        in_specs=[SMEM] * 5 + [HBM, HBM] + [VMEM] * 3,
-        out_specs=[VMEM] * 3,
-        out_shape=[shape((NCH, NB, NB), f32), shape((3, Q, Q), bf16), shape((ROWS, LANES), f32)],
-        scratch_shapes=fetched,
+        in_specs=[SMEM] * 5 + [HBM, HBM] + [VMEM] * 4,
+        out_specs=[VMEM, VMEM, VMEM, HBM],
+        out_shape=[shape((NCH, NB, NB), f32), shape((3, Q, Q), bf16), shape((ROWS, LANES), f32), shape((2, HALF, HALF), bf16)],
+        scratch_shapes=[*fetched, pltpu.VMEM((2, HALF, HALF), bf16), pltpu.SemaphoreType.DMA],
         compiler_params=PARAMS,
         name="side",
     )(
         place, own_mix, cross_mix, shells, partner, vertex, loop_matrix, grid_index.reshape(1, Q),
-        shells.reshape(TILE_COLS, LANES), partner.reshape(TILE_COLS, LANES),
+        shells.reshape(TILE_COLS, LANES), partner.reshape(TILE_COLS, LANES), partner_row,
     )
     back = pl.pallas_call(
         lattice_kernel,
@@ -258,7 +262,7 @@
         scratch_shapes=[pltpu.VMEM((NCH, NB, NB), bf16), pltpu.SemaphoreType.DMA((NCH,))],
         compiler_params=PARAMS,
         name="flow",
-    )(received, vertex_sum, partner_row)
+    )(received, vertex_sum, blocks)
 
 
 def solution(mesh):

time: 116 us -> 116 us (level)
    unnamed x18 -> x22, local copies, waits for them, and re-layouts: 5.08 us -> 5.79 us
where the time goes in v5:
time: 116 us
  blocking collectives  48.4 us (42%)
  waiting for transfers between devices  31.6 us (27%)
  starting transfers between devices  15.7 us (14%)
  Pallas kernels  14.6 us (13%)
  local copies, waits for them, and re-layouts  5.79 us (5%)
    all_to_all x1, blocking collectives, per_device(): received = lax.all_to_all(back, AXES, 0, 0, tiled=True).reshape(TILES)  48.4 us
    all_to_all x1, waiting for transfers between devices, per_device(): lax.all_to_all(sent.reshape(Q, NCH, SUB, LANES), AXES, 0, 0, tiled=True)  31.6 us
    all_to_all x1, starting transfers between devices, per_device(): lax.all_to_all(sent.reshape(Q, NCH, SUB, LANES), AXES, 0, 0, tiled=True)  15.7 us
    unnamed x22, local copies, waits for them, and re-layouts  5.79 us
    pallas_call x1, Pallas kernels, per_device(): pl.pallas_call(product_kernel, grid=(NCH,), in_specs=[matrix_spec, matrix...  5.62 us
    pallas_call x1, Pallas kernels, per_device(): pl.pallas_call(side_kernel, in_specs=[SMEM] * 5 + [HBM, HBM] + [VMEM] * 4...  3.69 us
    pallas_call x1, Pallas kernels, per_device(): pl.pallas_call(lattice_kernel, in_specs=[VMEM] * 3, out_specs=VMEM, out_s...  3.54 us
  transfers between devices with their start and end apart: 1, of which 1 were waited for; matrix products, arithmetic and copies ran while one was open for 0% of the time, Pallas kernels for 3%

profile of v5, /device:TPU:1, one launch (start us, length us, event | category | flops | bytes accessed | tf_op | source)
XLA Modules:
  0.0 116.1 jit_solution(7996502913846751523)
XLA Ops:
  0.0 5.6 %product.1 = bf16[32,2,4,3,8,128]{5,4,3,2,1,0:T(8,128)(2,1)} custom-call(bf16[3,1,512,512]{3,2,1,0:T(8,128)(2,1)} %vertex_hbm.1, bf16[3,1,512,512]{3,2,1,0:T(8,128)(2,1)} %loop_hbm.1, s32[1,512]{1,0:T(1,128)} %bitcast.8), custom_call_target="tpu_custom_call" | custom-call | tf_op jit(solution)/shard_map/product/pallas_call | solution.py:224
  5.6 0.0 copy-start
  5.6 0.0 copy-start.6
  5.6 0.0 copy-start.7
  5.6 15.7 %all-to-all-start = ((bf16[256,3,8,128]{3,2,1,0:T(8,128)(2,1)}), bf16[256,3,8,128]{3,2,1,0:T(8,128)(2,1)S(1)}, u32[]{:S(2)}, u32[]{:S(2)}) async-start(bf16[256,3,8,128]{3,2,1,0:T(8,128)(2,1)} %bitcast.13), calls=%async_computation | async-start | bytes 3145728 | tf_op jit(solution)/shard_map/all_to_all | solution.py:234
  21.3 0.0 copy-done
  21.3 0.0 copy-done.6
  21.3 0.0 copy-done.7
  21.3 0.0 copy-start.1
  21.4 1.4 %copy-done.1 = bf16[3,1,512,512]{3,2,1,0:T(8,128)(2,1)S(1)} copy-done((bf16[3,1,512,512]{3,2,1,0:T(8,128)(2,1)S(1)}, bf16[3,1,512,512]{3,2,1,0:T(8,128)(2,1)}, u32[]{:S(2)}) %copy-start.1) | copy-done | bytes 1572888
  22.8 0.0 copy-start.8
  22.8 0.7 copy-done.8
  23.4 0.0 copy-start.9
  23.4 0.7 copy-done.9
  24.1 0.0 copy-start.10
  24.1 0.7 copy-done.10
  24.8 3.7 %side.1 = (f32[3,512,512]{2,1,0:T(8,128)S(1)}, bf16[3,256,256]{2,1,0:T(8,128)(2,1)S(1)}, f32[16,128]{1,0:T(8,128)S(1)}, bf16[2,256,256]{2,1,0:T(8,128)(2,1)S(1)}) custom-call(s32[1]{0:T(128)} %bitcast.2.place_ref, f32[3,3]{1,0:T(4,128)S(1)} %copy-done.8, f32[3,3]{1,0:T(4,128)S(1)} %copy-done.9, s32[512]{0:T(512)S(1)} %copy-done.7, s32[512]{0:T(512)S(1)} %copy-done.6, ...), custom_call_target="tpu_custom_call" | custom-call | tf_op jit(solution)/shard_map/side/pallas_call | solution.py:235
  28.5 0.0 copy-start.2
  28.5 1.6 %copy-done.2 = f32[3,512,512]{2,1,0:T(8,128)} copy-done((f32[3,512,512]{2,1,0:T(8,128)}, f32[3,512,512]{2,1,0:T(8,128)S(1)}, u32[]{:S(2)}) %copy-start.2) | copy-done | bytes 3145752
  30.1 0.0 copy-start.4
  30.1 0.7 copy-done.4
  30.8 31.6 %all-to-all-done.arrived_ref = bf16[256,3,8,128]{3,2,1,0:T(8,128)(2,1)S(1)} async-done(((bf16[256,3,8,128]{3,2,1,0:T(8,128)(2,1)}), bf16[256,3,8,128]{3,2,1,0:T(8,128)(2,1)S(1)}, u32[]{:S(2)}, u32[]{:S(2)}) %all-to-all-start) | async-done | bytes 1572896 | tf_op jit(solution)/shard_map/all_to_all | solution.py:234
  62.4 0.0 copy-start.5
  62.4 3.5 %lattice.1 = bf16[256,3,8,128]{3,2,1,0:T(8,128)(2,1)S(1)} custom-call(bf16[256,3,8,128]{3,2,1,0:T(8,128)(2,1)S(1)} %all-to-all-done.arrived_ref, bf16[3,256,256]{2,1,0:T(8,128)(2,1)S(1)} %get-tuple-element.9.squares_ref, f32[16,128]{1,0:T(8,128)S(1)} %get-tuple-element.10.rows_ref), custom_call_target="tpu_custom_call" | custom-call | tf_op jit(solution)/shard_map/lattice/pallas_call | solution.py:247
  66.0 0.0 copy-start.3
  66.0 48.4 %all_to_all.10 = bf16[256,3,8,128]{3,2,1,0:T(8,128)(2,1)S(1)} all-to-all(bf16[256,3,8,128]{3,2,1,0:T(8,128)(2,1)S(1)} %lattice.1), channel_id=1, replica_groups=mesh['mom'=16,'bond'=16] {'mom','bond'}, dimensions={0} | all-to-all | bytes 3145728 | tf_op jit(solution)/shard_map/all_to_all | solution.py:256
  114.3 0.0 copy-done.5
  114.3 0.0 copy-done.3
  114.3 1.8 %flow.1 = bf16[3,1,512,512]{3,2,1,0:T(8,128)(2,1)} custom-call(bf16[32,2,4,3,8,128]{5,4,3,2,1,0:T(8,128)(2,1)S(1)} %bitcast.7, f32[3,512,512]{2,1,0:T(8,128)S(1)} %copy-done.3, bf16[2,256,256]{2,1,0:T(8,128)(2,1)S(1)} %copy-done.5), custom_call_target="tpu_custom_call" | custom-call | tf_op jit(solution)/shard_map/flow/pallas_call | solution.py:257
Async XLA Ops:
  5.6 15.7 %copy-start = (bf16[3,1,512,512]{3,2,1,0:T(8,128)(2,1)S(1)}, bf16[3,1,512,512]{3,2,1,0:T(8,128)(2,1)}, u32[]{:S(2)}) copy-start(bf16[3,1,512,512]{3,2,1,0:T(8,128)(2,1)} %vertex_hbm.1) | copy-start | bytes 4718596
  5.6 15.7 %copy-start.6 = (s32[512]{0:T(512)S(1)}, s32[512]{0:T(512)}, u32[]{:S(2)}) copy-start(s32[512]{0:T(512)} %partner_s.1) | copy-start | bytes 6148
  5.6 15.7 %copy-start.7 = (s32[512]{0:T(512)S(1)}, s32[512]{0:T(512)}, u32[]{:S(2)}) copy-start(s32[512]{0:T(512)} %shells_s.1) | copy-start | bytes 6148
  5.6 56.8 %all-to-all-start = ((bf16[256,3,8,128]{3,2,1,0:T(8,128)(2,1)}), bf16[256,3,8,128]{3,2,1,0:T(8,128)(2,1)S(1)}, u32[]{:S(2)}, u32[]{:S(2)}) async-start(bf16[256,3,8,128]{3,2,1,0:T(8,128)(2,1)} %bitcast.13), calls=%async_computation | async-start | bytes 3145728 | tf_op jit(solution)/shard_map/all_to_all | solution.py:234
  21.3 1.4 %copy-start.1 = (bf16[3,1,512,512]{3,2,1,0:T(8,128)(2,1)S(1)}, bf16[3,1,512,512]{3,2,1,0:T(8,128)(2,1)}, u32[]{:S(2)}) copy-start(bf16[3,1,512,512]{3,2,1,0:T(8,128)(2,1)} %loop_hbm.1) | copy-start | bytes 4718596
  22.8 0.7 copy-start.8
  23.4 0.7 copy-start.9
  24.1 0.7 copy-start.10
  28.5 1.6 %copy-start.2 = (f32[3,512,512]{2,1,0:T(8,128)}, f32[3,512,512]{2,1,0:T(8,128)S(1)}, u32[]{:S(2)}) copy-start(f32[3,512,512]{2,1,0:T(8,128)S(1)} %get-tuple-element.11.sum_ref) | copy-start | bytes 9437188
  30.1 0.7 copy-start.4
  62.4 51.9 %copy-start.5 = (bf16[2,256,256]{2,1,0:T(8,128)(2,1)S(1)}, bf16[2,256,256]{2,1,0:T(8,128)(2,1)}, u32[]{:S(2)}) copy-start(bf16[2,256,256]{2,1,0:T(8,128)(2,1)} %copy-done.4) | copy-start | bytes 786436
  66.0 48.4 %copy-start.3 = (f32[3,512,512]{2,1,0:T(8,128)S(1)}, f32[3,512,512]{2,1,0:T(8,128)}, u32[]{:S(2)}) copy-start(f32[3,512,512]{2,1,0:T(8,128)} %copy-done.2) | copy-start | bytes 9437188
